TPU v7x, 256 devices: a whole 4x4x8 slice. The times are simulated.
256 devices in a mesh: seq: 16 (over z, core), section: 4 (over y), tp: 4 (over x).
Axes of the slice: x: 4, y: 4, z: 8, core: 2. Of those that a mesh axis runs over, the one named last changes fastest.
Arguments:
- h_in: bfloat16 [4, 4096, 3072], P('section', 'seq', 'tp'), may hold values from -32 to 32
- memory: bfloat16 [4, 4096, 3072], P('section', 'seq', 'tp'), may hold values from -32 to 32
- cotangent: bfloat16 [4, 4096, 3072], P('section', 'seq', 'tp'), may hold values from -6 to 6
- block_docs: int32 [4, 32], P('section', 'seq'), may hold values from 0 to 3, never falling along the last dimension, each value on 1 to 24 neighbouring positions
- w_query: bfloat16 [4, 3072, 1536], P('section', None, 'tp'), may hold values from -0.109375 to 0.109375
- w_out: bfloat16 [4, 1536, 3072], P('section', 'tp'), may hold values from -0.15625 to 0.15625
- self_key_value_weight: bfloat16 [3072, 2, 512], P(None, None, 'tp'), may hold values from -0.109375 to 0.109375
- cache_key_value_weight: bfloat16 [3072, 2, 512], P(None, None, 'tp'), may hold values from -0.109375 to 0.109375
Outputs:
- passed_forward: bfloat16 [4, 4096, 3072], P('section', 'seq', 'tp')
- grad_input: bfloat16 [4, 4096, 3072], P('section', 'seq', 'tp')
- grad_memory: bfloat16 [4, 4096, 3072], P('section', 'seq', 'tp')
- grad_w_query: float32 [4, 3072, 1536], P('section', 'seq', 'tp')
- grad_w_out: float32 [4, 1536, 3072], P('section', 'tp', 'seq')
- grad_w_self_kv: float32 [3072, 2, 512], P(('seq', 'section'), None, 'tp')
- grad_w_cache: float32 [3072, 2, 512], P(('seq', 'section'), None, 'tp')
Inputs may be any that keep to these rules, and one draw needn't show every extreme that they name: block_docs[s, b] is the document of tokens b * 128 to b * 128 + 127 of section s; numbers never fall along a row, and in every row one document spans exactly 24 blocks.
All inputs are finite; a program needn't handle non-finite values.
Results may differ from a plain program's by a relative error of at most 0.02.
Values may be sent and summed in bfloat16 or wider, within the bound.
A program may use at most 128 MiB of HBM per device.

v0:
```python
import math

import jax
import jax.numpy as jnp
from jax import lax
from jax.sharding import PartitionSpec as P

HEAD_DIM = 128
BLK = 128
WIN = 1024


score_scale = 40.0
norm_eps = 1e-06


def passed_along(value, axis, steps):
    count = lax.axis_size(axis)
    pairs = [(source, (source + steps) % count) for source in range(count)]
    return lax.ppermute(value, axis, pairs)


def row_norm(values):
    wide_vals = values.astype(jnp.float32)
    factor = lax.rsqrt(jnp.mean(wide_vals * wide_vals, axis=-1) + norm_eps)
    return ((wide_vals * factor[:, None]).astype(jnp.bfloat16), factor)


def unit_rows(values):
    return values * lax.rsqrt(jnp.sum(values * values, axis=-1, keepdims=True) + norm_eps)


def visible(query_pos, query_doc, key_pos, key_doc, self_section):
    upper_bound = jnp.where(self_section, query_pos, query_pos // BLK * BLK + BLK - 1)
    lower_bound = jnp.where(self_section, query_pos - WIN, -1)
    same_doc = query_doc[:, None] == key_doc[None, :]
    return (
        same_doc
        & (key_pos[None, :] <= upper_bound[:, None])
        & (key_pos[None, :] > lower_bound[:, None])
    )


def contract_rows(left, right):
    return lax.dot_general(
        left, right, (((0,), (0,)), ((), ())), preferred_element_type=jnp.float32
    )


def contract_cols(left, right):
    return lax.dot_general(
        left, right, (((1,), (1,)), ((), ())), preferred_element_type=jnp.float32
    )


def on_device(
    h_in,
    memory,
    cotangent,
    block_docs,
    w_query,
    w_out,
    self_key_value_weight,
    cache_key_value_weight,
):
    section_id = lax.axis_index("section")
    shard_id = lax.axis_index("seq")
    self_section = section_id == 0
    hidden = h_in[0]
    source = jnp.where(self_section, hidden, memory[0])
    full_rows, full_source = (
        lax.all_gather(hidden, "tp", axis=1, tiled=True),
        lax.all_gather(source, "tp", axis=1, tiled=True),
    )
    row_count = hidden.shape[0]
    hidden_model_width = full_rows.shape[1]
    normalized_input, row_factor = row_norm(full_rows)
    normalized_source, source_factor = row_norm(full_source)
    query_projection_weight = w_query[0]
    out_weight = w_out[0]
    key_value_matrix = jnp.where(self_section, self_key_value_weight, cache_key_value_weight)
    kv_heads = self_key_value_weight.shape[2] // HEAD_DIM
    query_heads = query_projection_weight.shape[1] // HEAD_DIM
    query_group_width = query_heads // kv_heads
    key_value_flattened = key_value_matrix.reshape(hidden_model_width, 2 * kv_heads * HEAD_DIM)
    query_matrix = jnp.dot(
        normalized_input, query_projection_weight, preferred_element_type=jnp.float32
    ).reshape(row_count, kv_heads, query_group_width, HEAD_DIM)
    key_value_pairs = jnp.dot(
        normalized_source, key_value_flattened, preferred_element_type=jnp.float32
    ).reshape(row_count, 2, kv_heads, HEAD_DIM)
    query_unit = unit_rows(query_matrix).astype(jnp.bfloat16)
    key_raw = key_value_pairs[:, 0]
    key_unit = unit_rows(key_raw).astype(jnp.bfloat16)
    value_bf = key_value_pairs[:, 1].astype(jnp.bfloat16)
    packed = jnp.stack([key_unit, value_bf], axis=1).reshape(row_count, 2, kv_heads * HEAD_DIM)
    all_kv, all_docs = (
        lax.all_gather(packed, "seq", axis=0, tiled=True),
        lax.all_gather(block_docs[0], "seq", axis=0, tiled=True),
    )
    sequence_length_total = all_kv.shape[0]
    span_len = math.gcd(sequence_length_total, 512)
    block_count = sequence_length_total // span_len
    key_all = all_kv[:, 0].reshape(block_count, span_len, kv_heads, HEAD_DIM)
    value_all = all_kv[:, 1].reshape(block_count, span_len, kv_heads, HEAD_DIM)
    key_doc_all = jnp.repeat(all_docs, BLK).reshape(block_count, span_len)
    key_pos_all = jnp.arange(sequence_length_total, dtype=jnp.int32).reshape(block_count, span_len)
    query_pos = shard_id * row_count + jnp.arange(row_count, dtype=jnp.int32)
    query_doc = jnp.repeat(block_docs[0], BLK)

    def block_scores(key_block, key_pos, key_doc):
        allowed = visible(query_pos, query_doc, key_pos, key_doc, self_section)[:, None, None, :]
        scores = score_scale * jnp.einsum(
            "tgjd,ugd->tgju", query_unit, key_block, preferred_element_type=jnp.float32
        )
        return (allowed, scores)

    def forward_step(running, pieces):
        numerator, softmax_denominator = running
        key_block, value_block, key_pos, key_doc = pieces
        allowed, scores = block_scores(key_block, key_pos, key_doc)
        weights = jnp.where(allowed, jnp.exp(scores), 0.0)
        softmax_denominator = softmax_denominator + jnp.sum(weights, axis=-1)
        numerator = numerator + jnp.einsum(
            "tgju,ugd->tgjd",
            weights.astype(jnp.bfloat16),
            value_block,
            preferred_element_type=jnp.float32,
        )
        return ((numerator, softmax_denominator), None)

    start_num = jnp.zeros((row_count, kv_heads, query_group_width, HEAD_DIM), jnp.float32)
    start_den = jnp.zeros((row_count, kv_heads, query_group_width), jnp.float32)
    (numerator, softmax_denominator), _ = lax.scan(
        forward_step, (start_num, start_den), (key_all, value_all, key_pos_all, key_doc_all)
    )
    attention_output = (numerator / softmax_denominator[..., None]).astype(jnp.bfloat16)
    attn_flat = attention_output.reshape(row_count, query_heads * HEAD_DIM)
    projected = jnp.dot(attn_flat, out_weight, preferred_element_type=jnp.float32)
    projected = lax.psum_scatter(
        projected.astype(jnp.bfloat16), "tp", scatter_dimension=1, tiled=True
    ).astype(jnp.float32)
    h_out = (hidden.astype(jnp.float32) + projected).astype(jnp.bfloat16)
    passed = passed_along(h_out, "section", 1)
    grad_local = cotangent[0]
    grad_rows = lax.all_gather(grad_local, "tp", axis=1, tiled=True)
    attention_gradient = (
        contract_cols(grad_rows, out_weight)
        .astype(jnp.bfloat16)
        .reshape(row_count, kv_heads, query_group_width, HEAD_DIM)
    )
    delta = jnp.sum(
        attention_gradient.astype(jnp.float32) * attention_output.astype(jnp.float32), axis=-1
    )

    def backward_step(running, pieces):
        key_block, value_block, key_pos, key_doc = pieces
        allowed, scores = block_scores(key_block, key_pos, key_doc)
        probs = jnp.where(allowed, jnp.exp(scores) / softmax_denominator[..., None], 0.0)
        grad_probs = jnp.einsum(
            "tgjd,ugd->tgju", attention_gradient, value_block, preferred_element_type=jnp.float32
        )
        grad_scores = (probs * (grad_probs - delta[..., None])).astype(jnp.bfloat16)
        running = running + score_scale * jnp.einsum(
            "tgju,ugd->tgjd", grad_scores, key_block, preferred_element_type=jnp.float32
        )
        grad_key = score_scale * jnp.einsum(
            "tgju,tgjd->ugd", grad_scores, query_unit, preferred_element_type=jnp.float32
        )
        value_gradient = jnp.einsum(
            "tgju,tgjd->ugd",
            probs.astype(jnp.bfloat16),
            attention_gradient,
            preferred_element_type=jnp.float32,
        )
        return (running, jnp.stack([grad_key, value_gradient], axis=1))

    query_gradient, kv_terms = lax.scan(
        backward_step, jnp.zeros_like(start_num), (key_all, value_all, key_pos_all, key_doc_all)
    )
    kv_terms = kv_terms.reshape(sequence_length_total, 2, kv_heads * HEAD_DIM)
    kv_grads = lax.psum_scatter(
        kv_terms.astype(jnp.bfloat16), "seq", scatter_dimension=0, tiled=True
    ).astype(jnp.float32)
    _, query_pull = jax.vjp(unit_rows, query_matrix)
    grad_queries = (
        query_pull(query_gradient)[0]
        .reshape(row_count, query_heads * HEAD_DIM)
        .astype(jnp.bfloat16)
    )
    _, key_pull = jax.vjp(unit_rows, key_raw)
    key_gradient_rows = key_pull(kv_grads[:, 0].reshape(row_count, kv_heads, HEAD_DIM))[0]
    grad_values = kv_grads[:, 1].reshape(row_count, kv_heads, HEAD_DIM)
    key_value_gradient = (
        jnp.stack([key_gradient_rows, grad_values], axis=1)
        .reshape(row_count, 2 * kv_heads * HEAD_DIM)
        .astype(jnp.bfloat16)
    )
    back_rows = contract_cols(grad_queries, query_projection_weight)
    back_source = contract_cols(key_value_gradient, key_value_flattened)
    rows_part, source_part = (
        lax.psum_scatter(
            back_rows.astype(jnp.bfloat16), "tp", scatter_dimension=1, tiled=True
        ).astype(jnp.float32),
        lax.psum_scatter(
            back_source.astype(jnp.bfloat16), "tp", scatter_dimension=1, tiled=True
        ).astype(jnp.float32),
    )
    hidden_wide = hidden.astype(jnp.float32)
    source_wide = source.astype(jnp.float32)
    row_dot = jnp.sum(rows_part * hidden_wide, axis=1)
    source_dot = jnp.sum(source_part * source_wide, axis=1)
    row_total, source_total = lax.psum((row_dot, source_dot), "tp")
    row_cube = row_factor * row_factor * row_factor
    source_cube = source_factor * source_factor * source_factor
    grad_input = (
        grad_local.astype(jnp.float32)
        + row_factor[:, None] * rows_part
        - hidden_wide * (row_cube * row_total / hidden_model_width)[:, None]
    )
    grad_memory = (
        source_factor[:, None] * source_part
        - source_wide * (source_cube * source_total / hidden_model_width)[:, None]
    )
    weight_share = lax.psum_scatter(
        jnp.stack(
            [contract_rows(normalized_input, grad_queries), contract_rows(grad_rows, attn_flat)],
            axis=1,
        ).astype(jnp.bfloat16),
        "seq",
        scatter_dimension=0,
        tiled=True,
    ).astype(jnp.float32)
    query_grad = weight_share[:, 0]
    out_grad_flip = weight_share[:, 1]
    product = contract_rows(normalized_source, key_value_gradient)
    shared = lax.psum_scatter(
        jnp.stack(
            [jnp.where(self_section, product, 0.0), jnp.where(self_section, 0.0, product)], axis=1
        ),
        ("seq", "section"),
        scatter_dimension=0,
        tiled=True,
    )
    share_rows = shared.shape[0]
    self_grad = shared[:, 0].reshape(share_rows, 2, kv_heads * HEAD_DIM)
    cache_grad = shared[:, 1].reshape(share_rows, 2, kv_heads * HEAD_DIM)
    return (
        passed[None],
        grad_input.astype(jnp.bfloat16)[None],
        grad_memory.astype(jnp.bfloat16)[None],
        query_grad[None],
        out_grad_flip.T[None],
        self_grad,
        cache_grad,
    )


def solution(mesh):
    return jax.shard_map(
        on_device,
        mesh=mesh,
        in_specs=(
            P("section", "seq", "tp"),
            P("section", "seq", "tp"),
            P("section", "seq", "tp"),
            P("section", "seq"),
            P("section", None, "tp"),
            P("section", "tp", None),
            P(None, None, "tp"),
            P(None, None, "tp"),
        ),
        out_specs=(
            P("section", "seq", "tp"),
            P("section", "seq", "tp"),
            P("section", "seq", "tp"),
            P("section", "seq", "tp"),
            P("section", "tp", "seq"),
            P(("seq", "section"), None, "tp"),
            P(("seq", "section"), None, "tp"),
        ),
        check_vma=False,
    )
```

profile of v0, /device:TPU:2, one launch (start us, length us, event | category | flops | bytes accessed | tf_op | source)
XLA Modules:
  0.0 663.4 jit_solution(13786835592352315193)
XLA Ops:
  16.6 24.2 %all-gather.16.cloned.1.call-done = bf16[1,256,3072]{2,1,0:T(8,128)(2,1)} async-done(((bf16[1,256,768]{2,1,0:T(8,128)(2,1)}), bf16[1,256,3072]{2,1,0:T(8,128)(2,1)}) %all-gather.16.cloned.1.call-update) | async-done | bytes 1572880 | tf_op jit(solution)/shard_map/all_gather | solution.py:73
  49.0 13.9 %all-reduce = s32[32]{0:T(128)S(1)} all-reduce(s32[32]{0:T(128)S(1)} %bitcast_dynamic-update-slice_fusion), channel_id=3, replica_groups=mesh['seq'=16,'section'=4,'tp'=4] {'seq'}, use_global_device_ids=true, to_apply=%add | all-reduce | flops 32 | bytes 256
  64.4 7.2 %all-gather.12.cloned.1.call-done = bf16[1,256,3072]{2,1,0:T(8,128)(2,1)} async-done(((bf16[1,256,768]{2,1,0:T(8,128)(2,1)}), bf16[1,256,3072]{2,1,0:T(8,128)(2,1)}) %all-gather.12.cloned.1.call-update) | async-done | bytes 1572880 | tf_op jit(solution)/shard_map/all_gather | solution.py:72
  76.3 26.1 %all-gather.14.cloned.1.call-done = bf16[1,256,3072]{2,1,0:T(8,128)(2,1)} async-done(((bf16[1,256,768]{2,1,0:T(8,128)(2,1)}), bf16[1,256,3072]{2,1,0:T(8,128)(2,1)}) %all-gather.14.cloned.1.call-update) | async-done | bytes 1572880 | tf_op jit(solution)/shard_map/all_gather | solution.py:146
  102.5 3.1 fusion.75
  105.9 39.8 %all-gather.10.cloned.1.call-done = bf16[4096,2,1,128]{0,3,1,2:T(8,128)(2,1)} async-done(((bf16[256,2,1,128]{0,3,1,2:T(8,128)(2,1)}), bf16[4096,2,1,128]{0,3,1,2:T(8,128)(2,1)}) %all-gather.10.cloned.1.call-update) | async-done | bytes 2097168 | tf_op jit(solution)/shard_map/all_gather | solution.py:98
  145.7 3.2 fusion.107
  153.5 42.5 %while.40 = (s32[]{:T(128)}, f32[256,1,3,128]{0,3,2,1:T(8,128)}, f32[256,1,3]{0,1,2:T(1,128)S(1)}, bf16[8,512,1,128]{1,3,2,0:T(8,128)(2,1)}, s32[8,512]{1,0:T(8,...) while((s32[]{:T(128)}, f32[256,1,3,128]{0,3,2,1:T(8,128)}, ...), condition=%wide.region_6.7_spmd.clone.clone.clone, body=%wide.region_4.6_spmd.clone.clone.clone.sunk | while | flops 203758080 | bytes 3113649 | solution.py:134
  199.1 2.7 copy.47
  203.3 74.2 %while.41 = (s32[]{:T(128)}, f32[256,1,3,128]{0,3,2,1:T(8,128)}, bf16[8,512,2,1,128]{4,1,2,3,0:T(8,128)(2,1)}, bf16[8,512,1,128]{3,1,2,0:T(8,128)(2,1)}, s32[8,5...) while((s32[]{:T(128)}, f32[256,1,3,128]{0,3,2,1:T(8,128)}, ...), condition=%wide.region_10.11_spmd.clone.clone.clone, body=%wide.region_9.10_spmd.clone.clone.clone.sunk | while | flops 507680512 | bytes 22703880 | solution.py:178
  277.5 4.5 copy.49
  282.0 4.2 convert_element_type.180
  290.0 55.7 %reduce-scatter.11.cloned.1.call-done = bf16[256,2,128]{0,2,1:T(8,128)(2,1)} async-done(((bf16[4096,2,128]{0,2,1:T(8,128)(2,1)}), bf16[256,2,128]{0,2,1:T(8,128)(2,1)}) %reduce-scatter.11.cloned.1.call-update) | async-done | bytes 131088 | tf_op jit(solution)/shard_map/reduce_scatter | solution.py:182
  346.7 3.2 convolution_convert_fusion.4
  350.9 3.8 convolution_convert_fusion.3
  358.5 2.8 pad_maximum_fusion.1
  364.1 3.1 pad_maximum_fusion
  367.3 6.4 reduce-scatter.9.cloned.1.call-done
  374.9 29.4 %reduce-scatter.13.cloned.1.call-done = bf16[256,768]{1,0:T(8,128)(2,1)} async-done(((bf16[256,3072]{1,0:T(8,128)(2,1)}), bf16[256,768]{1,0:T(8,128)(2,1)}) %reduce-scatter.13.cloned.1.call-update) | async-done | bytes 393232 | tf_op jit(solution)/shard_map/reduce_scatter | solution.py:205
  406.1 10.0 %all-reduce.1 = (f32[256]{0:T(256)}, f32[256]{0:T(256)}) all-reduce(f32[256]{0:T(256)S(1)} %fusion.90, f32[256]{0:T(256)} %fusion.88), channel_id=1, replica_groups=mesh['seq'=16,'section'=4,'tp'=4] {'tp'}, use_global_device_ids=true, to_apply=%region_14.15 | all-reduce | flops 512 | bytes 4096 | tf_op jit(solution)/shard_map/psum | solution.py:213
  416.8 18.1 %reduce-scatter.7.cloned.1.call-done = bf16[256,768]{1,0:T(8,128)(2,1)} async-done(((bf16[256,3072]{1,0:T(8,128)(2,1)}), bf16[256,768]{1,0:T(8,128)(2,1)}) %reduce-scatter.7.cloned.1.call-update) | async-done | bytes 393232 | tf_op jit(solution)/shard_map/reduce_scatter | solution.py:140
  439.6 9.2 %collective-permute-done = bf16[256,768]{1,0:T(8,128)(2,1)S(1)} collective-permute-done((bf16[256,768]{1,0:T(8,128)(2,1)S(1)}, bf16[256,768]{1,0:T(8,128)(2,1)S(1)}, u32[]{:S(2)}, u32[]{:S(2)}) %collective-permute-start) | collective-permute-done | bytes 393248 | tf_op jit(solution)/shard_map/ppermute | solution.py:20
  448.9 53.9 %reduce-scatter.15.cloned.1.call-done = bf16[192,2,384]{2,0,1:T(8,128)(2,1)} async-done(((bf16[3072,2,384]{2,0,1:T(8,128)(2,1)}), bf16[192,2,384]{2,0,1:T(8,128)(2,1)}) %reduce-scatter.15.cloned.1.call-update) | async-done | bytes 294928 | tf_op jit(solution)/shard_map/reduce_scatter | solution.py:225
  504.6 149.1 %reduce-scatter.17.cloned.1.call-done = f32[48,2,256]{2,0,1:T(8,128)} async-done(((f32[3072,2,256]{2,0,1:T(8,128)}), f32[48,2,256]{2,0,1:T(8,128)}) %reduce-scatter.17.cloned.1.call-update) | async-done | bytes 98320 | tf_op jit(solution)/shard_map/reduce_scatter | solution.py:237
  (344 shorter events, 173.6 us)
Async XLA Ops:
  7.2 67.0 %copy-start = (bf16[1,3072,384]{2,1,0:T(8,128)(2,1)S(1)}, bf16[1,3072,384]{2,1,0:T(8,128)(2,1)}, u32[]{:S(2)}) copy-start(bf16[1,3072,384]{2,1,0:T(8,128)(2,1)} %param.16) | copy-start | bytes 7077892
  7.2 33.6 %all-gather.16.cloned.1.call-start = ((), (), s32[]{:S(2)}) async-start(), calls=%async_computation.15 | async-start | bytes 1966080 | tf_op jit(solution)/shard_map/all_gather | solution.py:73
  9.2 62.4 %all-gather.12.cloned.1.call-start = ((), (), s32[]{:S(2)}) async-start(), calls=%async_computation.13 | async-start | bytes 1966080 | tf_op jit(solution)/shard_map/all_gather | solution.py:72
  10.0 92.5 %all-gather.14.cloned.1.call-start = ((), (), s32[]{:S(2)}) async-start(), calls=%async_computation.14 | async-start | bytes 1966080 | tf_op jit(solution)/shard_map/all_gather | solution.py:146
  10.7 135.0 %all-gather.10.cloned.1.call-start = ((), (), s32[]{:S(2)}) async-start(), calls=%async_computation.12 | async-start | bytes 2228224 | tf_op jit(solution)/shard_map/all_gather | solution.py:98
  42.7 4.2 copy-start.32
  46.9 298.8 %reduce-scatter.11.cloned.1.call-start = ((), (), s32[]{:S(2)}) async-start(), calls=%async_computation.8 | async-start | bytes 2228224 | tf_op jit(solution)/shard_map/reduce_scatter | solution.py:182
  105.8 43.2 %copy-start.12 = (bf16[256,384]{0,1:T(8,128)(2,1)}, bf16[256,384]{0,1:T(8,128)(2,1)S(1)}, u32[]{:S(2)}) copy-start(bf16[256,384]{0,1:T(8,128)(2,1)S(1)} %copy.43) | copy-start | bytes 589828
  199.1 2.7 copy-start.13
  286.3 87.4 %reduce-scatter.9.cloned.1.call-start = ((), (), s32[]{:S(2)}) async-start(), calls=%async_computation.7 | async-start | bytes 1966080 | tf_op jit(solution)/shard_map/reduce_scatter | solution.py:202
  289.7 56.9 %copy-start.18 = (f32[256,2,1,128]{0,3,1,2:T(8,128)S(1)}, f32[256,2,1,128]{0,3,1,2:T(8,128)}, u32[]{:S(2)}) copy-start(f32[256,2,1,128]{0,3,1,2:T(8,128)} %copy-done.17) | copy-start | bytes 786436
  289.7 56.9 %copy-start.24 = (f32[256]{0:T(256)S(1)}, f32[256]{0:T(256)}, u32[]{:S(2)}) copy-start(f32[256]{0:T(256)} %copy-done.23) | copy-start | bytes 3076
  289.7 56.9 %copy-start.22 = (f32[256]{0:T(256)S(1)}, f32[256]{0:T(256)}, u32[]{:S(2)}) copy-start(f32[256]{0:T(256)} %copy-done.21) | copy-start | bytes 3076
  289.8 114.5 %reduce-scatter.13.cloned.1.call-start = ((), (), s32[]{:S(2)}) async-start(), calls=%async_computation.9 | async-start | bytes 1966080 | tf_op jit(solution)/shard_map/reduce_scatter | solution.py:205
  350.0 84.9 %reduce-scatter.7.cloned.1.call-start = ((), (), s32[]{:S(2)}) async-start(), calls=%async_computation.6 | async-start | bytes 1966080 | tf_op jit(solution)/shard_map/reduce_scatter | solution.py:140
  354.7 148.0 %reduce-scatter.15.cloned.1.call-start = ((), (), s32[]{:S(2)}) async-start(), calls=%async_computation.10 | async-start | bytes 5013504 | tf_op jit(solution)/shard_map/reduce_scatter | solution.py:225
  361.3 292.4 %reduce-scatter.17.cloned.1.call-start = ((), (), s32[]{:S(2)}) async-start(), calls=%async_computation.11 | async-start | bytes 6389760 | tf_op jit(solution)/shard_map/reduce_scatter | solution.py:237
  367.2 6.5 copy-start.10
  367.2 37.0 %copy-start.8 = (bf16[1,256,768]{2,1,0:T(8,128)(2,1)S(1)}, bf16[1,256,768]{2,1,0:T(8,128)(2,1)}, u32[]{:S(2)}) copy-start(bf16[1,256,768]{2,1,0:T(8,128)(2,1)} %broadcast_select_fusion.2) | copy-start | bytes 1179652
  367.3 48.9 %copy-start.28 = (f32[256]{0:T(256)S(1)}, f32[256]{0:T(256)}, u32[]{:S(2)}) copy-start(f32[256]{0:T(256)} %copy-done.27) | copy-start | bytes 3076
  374.9 63.8 %copy-start.26 = (f32[256]{0:T(256)S(1)}, f32[256]{0:T(256)}, u32[]{:S(2)}) copy-start(f32[256]{0:T(256)} %copy-done.25) | copy-start | bytes 3076
  404.3 34.4 %copy-start.16 = (bf16[256,768]{1,0:T(8,128)(2,1)S(1)}, bf16[256,768]{1,0:T(8,128)(2,1)}, u32[]{:S(2)}) copy-start(bf16[256,768]{1,0:T(8,128)(2,1)} %reduce-scatter.13.cloned.1.call-done) | copy-start | bytes 1179652
  416.8 21.8 %copy-start.31 = (f32[256]{0:T(256)S(1)}, f32[256]{0:T(256)}, u32[]{:S(2)}) copy-start(f32[256]{0:T(256)} %get-tuple-element.984) | copy-start | bytes 3076
  437.2 11.7 %collective-permute-start = (bf16[256,768]{1,0:T(8,128)(2,1)S(1)}, bf16[256,768]{1,0:T(8,128)(2,1)S(1)}, u32[]{:S(2)}, u32[]{:S(2)}) collective-permute-start(bf16[256,768]{1,0:T(8,128)(2,1)S(1)} %get-tuple-element.1004), channel_id=1, source_target_pairs={{0,4},{4,8},{8,12},{12,0},{1,5},{5,9},{9,13},{13,1},{2,6},{6,10},{... | collective-permute-start | bytes 1179656 | tf_op jit(solution)/shard_map/ppermute | solution.py:20
  (34 other events, 53.5 us)
Sparse Core Ops, SparseCore 0:
  9.8 30.9 all-gather.15
  42.6 28.9 all-gather.11
  73.4 28.9 all-gather.13
  104.1 41.6 all-gather.9
  286.4 59.2 reduce-scatter.10
  348.1 25.5 reduce-scatter.8
  376.2 27.9 reduce-scatter.12
  406.8 27.9 reduce-scatter.6
  437.4 65.2 reduce-scatter.14
  506.8 146.8 reduce-scatter.16
where the time goes:
time: 667 us; the launch traced here: 663 us
  waiting for transfers between devices  421 us (63%)
  matrix products  94.9 us (14%)
  local copies, waits for them, and re-layouts  70.7 us (11%)
  other arithmetic  35.1 us (5%)
  blocking collectives  24 us (4%)
  between operations  15.2 us (2%)
    reduce_scatter x1, waiting for transfers between devices, on_device(): lax.psum_scatter(jnp.stack([jnp.where(self_section, product, 0.0), jnp.wh...  149 us
    reduce_scatter x1, waiting for transfers between devices, on_device(): lax.psum_scatter(kv_terms.astype(jnp.bfloat16), 'seq', scatter_dimension=...  55.7 us
    reduce_scatter x1, waiting for transfers between devices, on_device(): lax.psum_scatter(jnp.stack([contract_rows(normalized_input, grad_queries)...  53.9 us
    all_gather x1, waiting for transfers between devices, on_device(): lax.all_gather(packed, 'seq', axis=0, tiled=True)  39.8 us
    reduce_scatter x1, waiting for transfers between devices, on_device(): lax.psum_scatter(back_source.astype(jnp.bfloat16), 'tp', scatter_dimensio...  29.4 us
    all_gather x1, waiting for transfers between devices, on_device(): grad_rows = lax.all_gather(grad_local, 'tp', axis=1, tiled=True)  26.1 us
    all_gather x1, waiting for transfers between devices, on_device(): lax.all_gather(source, 'tp', axis=1, tiled=True)  24.2 us
    dot_general x16, matrix products, block_scores(): jnp.einsum('tgjd,ugd->tgju', query_unit, key_block, preferred_element_typ...  23 us
  transfers between devices with their start and end apart: 11, of which 11 were waited for; matrix products, arithmetic and copies ran while one was open for 8% of the time, Pallas kernels for 0%

commit v1 on v0

v1 whole, which is shorter than its diff:
```python
import functools
import math

import jax
import jax.numpy as jnp
from jax import lax
from jax.experimental import pallas as pl
from jax.experimental.pallas import tpu as pltpu
from jax.sharding import PartitionSpec as P

MESH = pl.DeviceIdType.MESH
HEAD_DIM = 128
BLK = 128
WIN = 1024
SCALE = 40.0
EPS = 1e-06
EXP2_SCALE = SCALE * math.log2(math.e)
F32 = jnp.float32
BF16 = jnp.bfloat16
DOC_ROWS = 16
VMEM_SPEC = pl.BlockSpec(memory_space=pltpu.VMEM)
ANY_SPEC = pl.BlockSpec(memory_space=pl.ANY)
SMEM_SPEC = pl.BlockSpec(memory_space=pltpu.SMEM)
VMEM_LIMIT = 60 * 1024 * 1024


def nt(left, right):
    return lax.dot_general(left, right, (((1,), (1,)), ((), ())), preferred_element_type=F32)


def nn(left, right):
    return lax.dot_general(left, right, (((1,), (0,)), ((), ())), preferred_element_type=F32)


def tn(left, right):
    return lax.dot_general(left, right, (((0,), (0,)), ((), ())), preferred_element_type=F32)


def remote(src, dst, send_sem, recv_sem, device):
    return pltpu.make_async_remote_copy(
        src_ref=src,
        dst_ref=dst,
        send_sem=send_sem,
        recv_sem=recv_sem,
        device_id=device,
        device_id_type=MESH,
    )


def greet(devices):
    barrier = pltpu.get_barrier_semaphore()
    for device in devices:
        pl.semaphore_signal(barrier, inc=1, device_id=device, device_id_type=MESH)
    pl.semaphore_wait(barrier, len(devices))


def run_together(*streams):
    live = list(streams)
    while live:
        for stream in list(live):
            try:
                next(stream)
            except StopIteration:
                live.remove(stream)


class Ring:
    def __init__(self, axis, count):
        self.axis = axis
        self.me = lax.axis_index(axis)
        self.count = count

    def at(self, step):
        return lax.rem(self.me + step + self.count, self.count)

    def device(self, step):
        return {self.axis: self.at(step)}


class Line:
    def __init__(self, count):
        self.me = lax.axis_index("seq")
        self.chips = count // 2
        self.chip = self.me // 2
        self.core = self.me - self.chip * 2
        self.other = 1 - self.core

    def chip_at(self, step):
        return lax.rem(self.chip + step + self.chips, self.chips)

    def index(self, step):
        return self.chip_at(step) * 2 + self.core

    def device(self, step):
        return {"seq": self.index(step)}

    def partner(self):
        return {"seq": self.chip * 2 + self.other}


def gather_four(ring, in_ref, out_ref, send, recv, local_sem):
    rows, width = in_ref.shape
    lo, hi = pl.ds(0, rows // 2), pl.ds(rows // 2, rows // 2)

    def cols(step):
        return pl.ds(pl.multiple_of(ring.at(step) * width, 128), width)

    def own(half, slot, step):
        return remote(
            in_ref.at[half, :], out_ref.at[half, cols(0)], send.at[slot], recv.at[slot], ring.device(step)
        )

    right_lo, left_hi = own(lo, 0, 1), own(hi, 1, -1)
    right_hi, left_lo = own(hi, 2, 1), own(lo, 3, -1)
    for copy in (right_lo, left_hi, right_hi, left_lo):
        copy.start()
    local = pltpu.make_async_copy(in_ref, out_ref.at[:, cols(0)], local_sem)
    local.start()
    yield
    right_lo.wait_recv()
    far_lo = out_ref.at[lo, cols(-1)]
    relay_right = remote(far_lo, far_lo, send.at[4], recv.at[4], ring.device(1))
    relay_right.start()
    left_hi.wait_recv()
    far_hi = out_ref.at[hi, cols(1)]
    relay_left = remote(far_hi, far_hi, send.at[5], recv.at[5], ring.device(-1))
    relay_left.start()
    yield
    for copy in (right_hi, left_lo, relay_right, relay_left):
        copy.wait_recv()
    local.wait()
    yield
    for copy in (right_lo, left_hi, right_hi, left_lo, relay_right, relay_left):
        copy.wait_send()


def gather_rows_kernel(count, src_ref, h_ref, cot_ref, src_out, h_out, cot_out, send, recv, local):
    ring = Ring("tp", count)
    greet([ring.device(1), ring.device(-1)])
    streams = [
        gather_four(ring, i, o, send.at[k], recv.at[k], local.at[k])
        for k, (i, o) in enumerate(((src_ref, src_out), (h_ref, h_out), (cot_ref, cot_out)))
    ]
    next(streams[0])
    for k in range(3):
        next(streams[k])
        if k < 2:
            next(streams[k + 1])
        next(streams[k])
    run_together(*streams)


def gather_rows(count, src, hidden, cot):
    rows, width = hidden.shape
    full = jax.ShapeDtypeStruct((rows, width * count), BF16)
    return pl.pallas_call(
        functools.partial(gather_rows_kernel, count),
        out_shape=(full, full, full),
        in_specs=[VMEM_SPEC] * 3,
        out_specs=[ANY_SPEC] * 3,
        scratch_shapes=[
            pltpu.SemaphoreType.DMA((3, 6)),
            pltpu.SemaphoreType.DMA((3, 6)),
            pltpu.SemaphoreType.DMA((3,)),
        ],
        compiler_params=pltpu.CompilerParams(collective_id=1, has_side_effects=True),
        name="gather_rows",
    )(src, hidden, cot)


def project_kernel(
    docs_ref, h_ref, src_ref, cot_ref, wq_ref, wo_ref, self_ref, cache_ref,
    q_ref, kv_ref, pay_ref, dout_ref, rh_ref, rs_ref,
    acc_q, acc_kv, acc_do, sum_h, sum_s,
):
    step = pl.program_id(0)
    steps = pl.num_programs(0)

    @pl.when(step == 0)
    def _():
        for ref in (acc_q, acc_kv, acc_do, sum_h, sum_s):
            ref[...] = jnp.zeros_like(ref)

    hidden, source = h_ref[...], src_ref[...]
    is_self = lax.axis_index("section") == 0
    weight = jnp.where(is_self, self_ref[...], cache_ref[...])
    acc_q[...] += nn(hidden, wq_ref[...])
    acc_kv[...] += nn(source, weight)
    acc_do[...] += nt(cot_ref[...], wo_ref[...])

    def squares(block):
        wide = block.astype(F32)
        wide = wide * wide
        parts = [wide[:, k : k + 128] for k in range(0, wide.shape[1], 128)]
        return functools.reduce(lambda a, b: a + b, parts)

    sum_h[...] += squares(hidden)
    sum_s[...] += squares(source)

    @pl.when(step == steps - 1)
    def _():
        width = h_ref.shape[1] * steps
        rh = lax.rsqrt(jnp.sum(sum_h[...], axis=1, keepdims=True) / width + EPS)
        rs = lax.rsqrt(jnp.sum(sum_s[...], axis=1, keepdims=True) / width + EPS)
        rh_ref[...] = jnp.broadcast_to(rh, rh_ref.shape)
        rs_ref[...] = jnp.broadcast_to(rs, rs_ref.shape)
        q_ref[...] = acc_q[...] * rh
        kv = acc_kv[...] * rs
        kv_ref[...] = kv
        key, value = kv[:, :HEAD_DIM], kv[:, HEAD_DIM:]
        unit = key * lax.rsqrt(jnp.sum(key * key, axis=1, keepdims=True) + EPS)
        rows = kv.shape[0]
        pay_ref[0:rows, 0:HEAD_DIM] = unit.astype(BF16)
        pay_ref[0:rows, HEAD_DIM:] = value.astype(BF16)
        lane = lax.broadcasted_iota(jnp.int32, (DOC_ROWS, 2 * BLK), 1)
        docs = jnp.where(lane < BLK, docs_ref[0, 0], docs_ref[0, 1])
        pay_ref[rows:, :] = docs.astype(F32).astype(BF16)
        dout_ref[...] = acc_do[...].astype(BF16)


def project(steps, docs, full_h, full_s, full_c, wq, wo, self_w, cache_w):
    rows, width = full_h.shape
    block = width // steps
    heads, kv = wq.shape[1], self_w.shape[1]
    by_col = pl.BlockSpec((rows, block), lambda i: (0, i))
    whole = lambda shape: pl.BlockSpec(shape, lambda i: (0, 0))
    return pl.pallas_call(
        project_kernel,
        grid=(steps,),
        out_shape=(
            jax.ShapeDtypeStruct((rows, heads), F32),
            jax.ShapeDtypeStruct((rows, kv), F32),
            jax.ShapeDtypeStruct((rows + DOC_ROWS, kv), BF16),
            jax.ShapeDtypeStruct((rows, heads), BF16),
            jax.ShapeDtypeStruct((rows, 128), F32),
            jax.ShapeDtypeStruct((rows, 128), F32),
        ),
        in_specs=[
            SMEM_SPEC, by_col, by_col, by_col,
            pl.BlockSpec((block, heads), lambda i: (i, 0)),
            pl.BlockSpec((heads, block), lambda i: (0, i)),
            pl.BlockSpec((block, kv), lambda i: (i, 0)),
            pl.BlockSpec((block, kv), lambda i: (i, 0)),
        ],
        out_specs=[
            whole((rows, heads)), whole((rows, kv)), whole((rows + DOC_ROWS, kv)),
            whole((rows, heads)), whole((rows, 128)), whole((rows, 128)),
        ],
        scratch_shapes=[
            pltpu.VMEM((rows, heads), F32), pltpu.VMEM((rows, kv), F32), pltpu.VMEM((rows, heads), F32),
            pltpu.VMEM((rows, 128), F32), pltpu.VMEM((rows, 128), F32),
        ],
        compiler_params=pltpu.CompilerParams(vmem_limit_bytes=VMEM_LIMIT),
        name="project",
    )(docs, full_h, full_s, full_c, wq, wo, self_w, cache_w)


def gather_keys_kernel(count, in_ref, out_ref, send, recv, to_core, from_core, local_sem):
    line = Line(count)
    rows = in_ref.shape[0]
    cut = (rows // 2 + 15) // 16 * 16
    halves = {1: pl.ds(0, cut), -1: pl.ds(cut, rows - cut)}
    greet([line.device(1), line.device(-1), line.partner()])
    copies = []

    def send_copy(src, dst, s, r, device):
        copy = remote(src, dst, s, r, device)
        copy.start()
        copies.append(copy)
        return copy

    last = line.chips // 2
    hops = {}
    for way, d in ((0, 1), (1, -1)):
        hops[way] = send_copy(
            in_ref, out_ref.at[line.me], send.at[way, 0], recv.at[way, 0], line.device(d)
        )
    passed = [
        send_copy(in_ref, out_ref.at[line.me], to_core.at[0], from_core.at[0], line.partner())
    ]
    local = pltpu.make_async_copy(in_ref, out_ref.at[line.me], local_sem)
    local.start()
    slot = 1
    for hop in range(1, last + 1):
        for way, d in ((0, 1), (1, -1)):
            hops[way].wait_recv()
            block = line.index(-d * hop)
            if hop < last:
                ahead = out_ref.at[block]
                if hop == last - 1:
                    ahead = out_ref.at[block, halves[d], :]
                hops[way] = send_copy(
                    ahead, ahead, send.at[way, hop], recv.at[way, hop], line.device(d)
                )
                piece = out_ref.at[block]
            else:
                piece = out_ref.at[block, halves[d], :]
            passed.append(
                send_copy(piece, piece, to_core.at[slot], from_core.at[slot], line.partner())
            )
            slot += 1
    for copy in passed:
        copy.wait_recv()
    local.wait()
    for copy in copies:
        copy.wait_send()


def gather_keys(count, payload):
    last = count // 4
    return pl.pallas_call(
        functools.partial(gather_keys_kernel, count),
        out_shape=jax.ShapeDtypeStruct((count,) + payload.shape, BF16),
        in_specs=[VMEM_SPEC],
        out_specs=ANY_SPEC,
        scratch_shapes=[
            pltpu.SemaphoreType.DMA((2, last)),
            pltpu.SemaphoreType.DMA((2, last)),
            pltpu.SemaphoreType.DMA((2 * last + 1,)),
            pltpu.SemaphoreType.DMA((2 * last + 1,)),
            pltpu.SemaphoreType.DMA,
        ],
        compiler_params=pltpu.CompilerParams(collective_id=2, has_side_effects=True),
        name="gather_keys",
    )(payload)


def attend_kernel(
    docs_ref, q_ref, dout_ref, kv_ref, wo_ref,
    attn_ref, proj_ref, gq_ref, dot_ref, dkv_ref,
    q_unit, dout, weights, acc, dq,
):
    seq = lax.axis_index("seq")
    is_self = lax.axis_index("section") == 0
    rows = q_ref.shape[0]
    heads = q_ref.shape[1] // HEAD_DIM
    chunks = kv_ref.shape[0]
    low = jnp.where(is_self, jnp.maximum(seq - WIN // rows, 0), 0)

    def head_rows(head):
        return pl.ds(head * rows, rows)

    def head_cols(head):
        return pl.ds(head * HEAD_DIM, HEAD_DIM)

    for head in range(heads):
        q = q_ref[:, head_cols(head)]
        unit = q * lax.rsqrt(jnp.sum(q * q, axis=1, keepdims=True) + EPS)
        q_unit[head_rows(head), :] = unit.astype(BF16)
    acc[...] = jnp.zeros_like(acc)
    dq[...] = jnp.zeros_like(dq)
    zero_chunk = jnp.zeros((rows, 2 * HEAD_DIM), BF16)

    @pl.loop(0, low)
    def _(j):
        dkv_ref[j] = zero_chunk

    @pl.loop(seq + 1, chunks)
    def _(j):
        dkv_ref[j] = zero_chunk

    row = lax.broadcasted_iota(jnp.int32, (rows, 1), 0)
    lane = lax.broadcasted_iota(jnp.int32, (1, rows), 1)
    query_doc = jnp.where(row < BLK, docs_ref[0, 0], docs_ref[0, 1]).astype(F32)
    query_pos = seq * rows + row
    upper = jnp.where(is_self, query_pos, query_pos // BLK * BLK + BLK - 1)
    lower = jnp.where(is_self, query_pos - WIN, -1)
    ones = jnp.ones((rows, HEAD_DIM), BF16)

    @pl.loop(low, seq + 1)
    def _(j):
        key = kv_ref[j, 0:rows, 0:HEAD_DIM]
        value = jnp.concatenate([kv_ref[j, 0:rows, HEAD_DIM:], ones], axis=1)
        key_doc = kv_ref[j, rows:, :].astype(F32)[0:1, :]
        key_pos = j * rows + lane
        seen = (key_doc == query_doc) & (key_pos <= upper) & (key_pos > lower)
        for head in range(heads):
            score = nt(q_unit[head_rows(head), :], key)
            weight = jnp.where(seen, jnp.exp2(score * EXP2_SCALE), 0.0).astype(BF16)
            weights[j, head_rows(head), :] = weight
            acc[head_rows(head), :] += nn(weight, value)

    deltas = []
    for head in range(heads):
        total = acc[head_rows(head), :]
        inverse = 1.0 / total[:, HEAD_DIM:]
        out = (total[:, :HEAD_DIM] * inverse).astype(BF16)
        attn_ref[:, head_cols(head)] = out
        grad = dout_ref[:, head_cols(head)].astype(F32)
        delta = jnp.sum(grad * out.astype(F32), axis=1, keepdims=True)
        dout[head_rows(head), :] = (grad * inverse).astype(BF16)
        deltas.append(delta * inverse[:, 0:1])

    @pl.loop(low, seq + 1)
    def _(j):
        key = kv_ref[j, 0:rows, 0:HEAD_DIM]
        value = kv_ref[j, 0:rows, HEAD_DIM:]
        grad_key = jnp.zeros((rows, HEAD_DIM), F32)
        grad_value = jnp.zeros((rows, HEAD_DIM), F32)
        for head in range(heads):
            weight = weights[j, head_rows(head), :]
            grad = dout[head_rows(head), :]
            grad_prob = nt(grad, value)
            grad_score = (weight.astype(F32) * (grad_prob - deltas[head])).astype(BF16)
            dq[head_rows(head), :] += nn(grad_score, key)
            grad_key += tn(grad_score, q_unit[head_rows(head), :])
            grad_value += tn(weight, grad)
        dkv_ref[j, :, 0:HEAD_DIM] = (SCALE * grad_key).astype(BF16)
        dkv_ref[j, :, HEAD_DIM:] = grad_value.astype(BF16)

    total = jnp.zeros((rows, 1), F32)
    for head in range(heads):
        q = q_ref[:, head_cols(head)]
        grad = SCALE * dq[head_rows(head), :]
        inverse = lax.rsqrt(jnp.sum(q * q, axis=1, keepdims=True) + EPS)
        along = jnp.sum(q * grad, axis=1, keepdims=True)
        back = (inverse * grad - q * (inverse * inverse * inverse * along)).astype(BF16)
        gq_ref[:, head_cols(head)] = back
        total += jnp.sum(back.astype(F32) * q, axis=1, keepdims=True)
    dot_ref[...] = jnp.broadcast_to(total, dot_ref.shape)
    attn = attn_ref[...]
    width = wo_ref.shape[1]
    piece = 768 if width % 768 == 0 else width
    for first in range(0, width, piece):
        span = pl.ds(first, piece)
        proj_ref[:, span] = nn(attn, wo_ref[:, span]).astype(BF16)


def attend(docs, q, dout, all_kv, wo):
    rows, cols = q.shape
    heads = cols // HEAD_DIM
    chunks = all_kv.shape[0]
    return pl.pallas_call(
        attend_kernel,
        out_shape=(
            jax.ShapeDtypeStruct((rows, cols), BF16),
            jax.ShapeDtypeStruct((rows, wo.shape[1]), BF16),
            jax.ShapeDtypeStruct((rows, cols), BF16),
            jax.ShapeDtypeStruct((rows, 128), F32),
            jax.ShapeDtypeStruct((chunks, rows, 2 * HEAD_DIM), BF16),
        ),
        in_specs=[SMEM_SPEC] + [VMEM_SPEC] * 4,
        out_specs=[VMEM_SPEC] * 5,
        scratch_shapes=[
            pltpu.VMEM((heads * rows, HEAD_DIM), BF16),
            pltpu.VMEM((heads * rows, HEAD_DIM), BF16),
            pltpu.VMEM((chunks, heads * rows, rows), BF16),
            pltpu.VMEM((heads * rows, 2 * HEAD_DIM), F32),
            pltpu.VMEM((heads * rows, HEAD_DIM), F32),
        ],
        compiler_params=pltpu.CompilerParams(vmem_limit_bytes=VMEM_LIMIT),
        name="attend",
    )(docs, q, dout, all_kv, wo)


def scatter_four(ring, in_ref, buf, stage, send, recv, finish):
    rows = in_ref.shape[0]
    width = in_ref.shape[1] // ring.count
    lo, hi = pl.ds(0, rows // 2), pl.ds(rows // 2, rows // 2)

    def block(half, step):
        return in_ref.at[half, pl.ds(pl.multiple_of(ring.at(step) * width, 128), width)]

    def move(src, slot, step):
        copy = remote(src, buf.at[slot], send.at[slot], recv.at[slot], ring.device(step))
        copy.start()
        return copy

    copies = [
        move(block(lo, 2), 0, 1),
        move(block(hi, 2), 1, -1),
        move(block(hi, 1), 2, 1),
        move(block(lo, -1), 3, -1),
    ]
    yield
    copies[0].wait_recv()
    stage[0] = (buf[0].astype(F32) + block(lo, 1)[...].astype(F32)).astype(BF16)
    copies.append(move(stage.at[0], 4, 1))
    yield
    copies[1].wait_recv()
    stage[1] = (buf[1].astype(F32) + block(hi, -1)[...].astype(F32)).astype(BF16)
    copies.append(move(stage.at[1], 5, -1))
    yield
    copies[2].wait_recv()
    copies[5].wait_recv()
    finish(hi, block(hi, 0)[...].astype(F32) + buf[2].astype(F32) + buf[5].astype(F32))
    yield
    copies[3].wait_recv()
    copies[4].wait_recv()
    finish(lo, block(lo, 0)[...].astype(F32) + buf[3].astype(F32) + buf[4].astype(F32))
    yield
    for copy in copies:
        copy.wait_send()


def scatter_four_scratch(rows, width):
    return [
        pltpu.VMEM((6, rows // 2, width), BF16),
        pltpu.VMEM((2, rows // 2, width), BF16),
        pltpu.SemaphoreType.DMA((6,)),
        pltpu.SemaphoreType.DMA((6,)),
    ]


def scatter_line(line, in_ref, other, buf, stage, send, recv, to_core, from_core, finish):
    rows = in_ref.shape[2]
    last = line.chips // 2
    halves = (pl.ds(0, rows // 2), pl.ds(rows // 2, rows // 2))
    order = [last]
    for k in range(last - 1, 0, -1):
        order += [k, -k]
    order.append(0)
    pieces = {}
    copies = []
    for slot, step in enumerate(order):
        chip = line.chip_at(step)
        copy = remote(
            in_ref.at[chip, line.other], other.at[chip], to_core.at[slot], from_core.at[slot], line.partner()
        )
        copy.start()
        copies.append(copy)
        pieces[step] = copy
    yield
    ready = set()

    def own(step, half):
        if abs(step) == last:
            step = last
        if step not in ready:
            pieces[step].wait_recv()
            ready.add(step)
        chip = line.chip_at(step)
        return in_ref[chip, line.core, half, :].astype(F32) + other[chip, half, :].astype(F32)

    sent = {}
    plan = [(last, 0)]
    for k in range(last - 1, 0, -1):
        plan += [(k, 1), (k, 0)]
    for k, which in plan:
        for way, d in ((0, 1), (1, -1)):
            part = which if way == 0 else 1 - which
            half = halves[part]
            value = own(d * k, half)
            if (way, k + 1, part) in sent:
                sent[way, k + 1, part].wait_recv()
                value = value + buf[way, k, half, :].astype(F32)
            stage[way, k - 1, half, :] = value.astype(BF16)
            copy = remote(
                stage.at[way, k - 1, half, :],
                buf.at[way, k - 1, half, :],
                send.at[way, k - 1, part],
                recv.at[way, k - 1, part],
                line.device(d),
            )
            copy.start()
            sent[way, k, part] = copy
            copies.append(copy)
            yield
    for part in (1, 0):
        half = halves[part]
        value = own(0, half)
        for way in (0, 1):
            sent[way, 1, part].wait_recv()
            value = value + buf[way, 0, half, :].astype(F32)
        finish(half, value)
        yield
    for copy in copies:
        copy.wait_send()


def scatter_line_scratch(chips, rows, width):
    last = chips // 2
    return [
        pltpu.VMEM((chips, rows, width), BF16),
        pltpu.VMEM((2, last, rows, width), BF16),
        pltpu.VMEM((2, last, rows, width), BF16),
        pltpu.SemaphoreType.DMA((2, last, 2)),
        pltpu.SemaphoreType.DMA((2, last, 2)),
        pltpu.SemaphoreType.DMA((chips,)),
        pltpu.SemaphoreType.DMA((chips,)),
    ]


def reduce_first_kernel(tp, seq, proj_ref, h_ref, dkv_ref, hout_ref, sum_ref, *scratch):
    four, rest = scratch[:4], scratch[4:]
    ring, line = Ring("tp", tp), Line(seq)
    greet([ring.device(1), ring.device(-1), line.device(1), line.device(-1), line.partner()])

    def finish_rows(half, value):
        hout_ref[half, :] = (h_ref[half, :].astype(F32) + value).astype(BF16)

    def finish_keys(half, value):
        sum_ref[half, :] = value

    run_together(
        scatter_line(line, dkv_ref, *rest, finish_keys),
        scatter_four(ring, proj_ref, *four, finish_rows),
    )


def reduce_first(tp, seq, proj, hidden, dkv):
    rows, width = hidden.shape
    chips = seq // 2
    dkv = dkv.reshape((chips, 2) + dkv.shape[1:])
    return pl.pallas_call(
        functools.partial(reduce_first_kernel, tp, seq),
        out_shape=(
            jax.ShapeDtypeStruct((rows, width), BF16),
            jax.ShapeDtypeStruct(dkv.shape[2:], F32),
        ),
        in_specs=[VMEM_SPEC] * 3,
        out_specs=[VMEM_SPEC] * 2,
        scratch_shapes=scatter_four_scratch(rows, width) + scatter_line_scratch(chips, *dkv.shape[2:]),
        compiler_params=pltpu.CompilerParams(
            collective_id=3, has_side_effects=True, vmem_limit_bytes=VMEM_LIMIT
        ),
        name="reduce_first",
    )(proj, hidden, dkv)


def backward_kernel(
    h_ref, src_ref, cot_ref, wq_ref, self_ref, cache_ref, gq_ref, dot_ref, attn_ref, kv_ref, sum_ref, rh_ref, rs_ref,
    rows_ref, source_ref, weight_ref,
    gkv, scaled_q, scaled_kv, fix_h, fix_s,
):
    step = pl.program_id(0)
    width = h_ref.shape[1] * pl.num_programs(0)

    @pl.when(step == 0)
    def _():
        kv, sums = kv_ref[...], sum_ref[...]
        key, grad = kv[:, :HEAD_DIM], sums[:, :HEAD_DIM]
        inverse = lax.rsqrt(jnp.sum(key * key, axis=1, keepdims=True) + EPS)
        along = jnp.sum(key * grad, axis=1, keepdims=True)
        back = inverse * grad - key * (inverse * inverse * inverse * along)
        both = jnp.concatenate([back, sums[:, HEAD_DIM:]], axis=1).astype(BF16)
        gkv[...] = both
        total = jnp.sum(both.astype(F32) * kv, axis=1, keepdims=True)
        rh, rs = rh_ref[:, 0:1], rs_ref[:, 0:1]
        fix_h[...] = rh_ref[...] * rh_ref[...] * dot_ref[...] / width
        fix_s[...] = rs_ref[...] * rs_ref[...] * total / width
        scaled_q[...] = (gq_ref[...].astype(F32) * rh).astype(BF16)
        scaled_kv[...] = (both.astype(F32) * rs).astype(BF16)

    hidden, source = h_ref[...], src_ref[...]
    is_self = lax.axis_index("section") == 0
    weight = jnp.where(is_self, self_ref[...], cache_ref[...])
    rh, rs = rh_ref[:, 0:1], rs_ref[:, 0:1]
    rows_ref[...] = (nt(gq_ref[...], wq_ref[...]) * rh - hidden.astype(F32) * fix_h[:, 0:1]).astype(BF16)
    source_ref[...] = (nt(gkv[...], weight) * rs - source.astype(F32) * fix_s[:, 0:1]).astype(BF16)
    cols = gq_ref.shape[1]
    weight_ref[:, 0:cols] = tn(hidden, scaled_q[...]).astype(BF16)
    weight_ref[:, cols : 2 * cols] = tn(cot_ref[...], attn_ref[...]).astype(BF16)
    weight_ref[:, 2 * cols :] = tn(source, scaled_kv[...]).astype(BF16)


def backward(steps, full_h, full_s, full_c, wq, self_w, cache_w, gq, dot, attn, kv, sums, rh, rs):
    rows, width = full_h.shape
    block = width // steps
    heads, kvw = wq.shape[1], self_w.shape[1]
    by_col = pl.BlockSpec((rows, block), lambda i: (0, i))
    by_row = lambda n: pl.BlockSpec((block, n), lambda i: (i, 0))
    whole = lambda n: pl.BlockSpec((rows, n), lambda i: (0, 0))
    return pl.pallas_call(
        backward_kernel,
        grid=(steps,),
        out_shape=(
            jax.ShapeDtypeStruct((rows, width), BF16),
            jax.ShapeDtypeStruct((rows, width), BF16),
            jax.ShapeDtypeStruct((width, 2 * heads + kvw), BF16),
        ),
        in_specs=[
            by_col, by_col, by_col, by_row(heads), by_row(kvw), by_row(kvw),
            whole(heads), whole(128), whole(heads), whole(kvw), whole(kvw), whole(128), whole(128),
        ],
        out_specs=[by_col, by_col, by_row(2 * heads + kvw)],
        scratch_shapes=[
            pltpu.VMEM((rows, kvw), BF16),
            pltpu.VMEM((rows, heads), BF16),
            pltpu.VMEM((rows, kvw), BF16),
            pltpu.VMEM((rows, 128), F32),
            pltpu.VMEM((rows, 128), F32),
        ],
        compiler_params=pltpu.CompilerParams(vmem_limit_bytes=VMEM_LIMIT),
        name="backward",
    )(full_h, full_s, full_c, wq, self_w, cache_w, gq, dot, attn, kv, sums, rh, rs)


def pass_along(ring, in_ref, out_ref, send, recv):
    copy = remote(in_ref, out_ref, send, recv, ring.device(1))
    copy.start()
    yield
    yield
    copy.wait()


def reduce_last_kernel(
    tp, seq, section, rows_ref, source_ref, weight_ref, hout_ref, cot_ref,
    passed_ref, gin_ref, gmem_ref, wq_ref, wo_ref, wself_ref, wcache_ref, *scratch
):
    four_a, four_b, rest = scratch[:4], scratch[4:8], scratch[8:15]
    pass_send, pass_recv, mine, got, ex_send, ex_recv, ex_local = scratch[15:]
    ring, line, sections = Ring("tp", tp), Line(seq), Ring("section", section)
    others = [sections.device(k) for k in range(1, section)]
    greet(
        [ring.device(1), ring.device(-1), line.device(1), line.device(-1), line.partner()] + others
    )
    heads = wq_ref.shape[1]

    def finish_input(half, value):
        gin_ref[half, :] = (cot_ref[half, :].astype(F32) + value).astype(BF16)

    def finish_memory(half, value):
        gmem_ref[half, :] = value.astype(BF16)

    def finish_weights(half, value):
        wq_ref[half, :] = value[:, 0:heads]
        wo_ref[half, :] = value[:, heads : 2 * heads]
        mine[half, :] = value[:, 2 * heads :]

    run_together(
        pass_along(sections, hout_ref, passed_ref, pass_send, pass_recv),
        scatter_line(line, weight_ref, *rest, finish_weights),
        scatter_four(ring, rows_ref, *four_a, finish_input),
        scatter_four(ring, source_ref, *four_b, finish_memory),
    )
    share = wself_ref.shape[0]
    copies = []
    for k in range(1, section):
        first = pl.multiple_of(sections.at(k) * share, 8)
        copy = remote(
            mine.at[pl.ds(first, share), :],
            got.at[sections.me],
            ex_send.at[k],
            ex_recv.at[k],
            sections.device(k),
        )
        copy.start()
        copies.append(copy)
    first = pl.multiple_of(sections.me * share, 8)
    local = pltpu.make_async_copy(mine.at[pl.ds(first, share), :], got.at[sections.me], ex_local)
    local.start()
    for copy in copies:
        copy.wait_recv()
    local.wait()
    wself_ref[...] = got[0]
    total = got[1]
    for k in range(2, section):
        total = total + got[k]
    wcache_ref[...] = total
    for copy in copies:
        copy.wait_send()


def reduce_last(tp, seq, section, rows_part, source_part, weight_part, hout, cot, heads, kvw):
    rows, width = hout.shape
    chips = seq // 2
    share = weight_part.shape[0] // seq
    weight_part = weight_part.reshape(chips, 2, share, weight_part.shape[1])
    piece = share // section
    return pl.pallas_call(
        functools.partial(reduce_last_kernel, tp, seq, section),
        out_shape=(
            jax.ShapeDtypeStruct((rows, width), BF16),
            jax.ShapeDtypeStruct((rows, width), BF16),
            jax.ShapeDtypeStruct((rows, width), BF16),
            jax.ShapeDtypeStruct((share, heads), F32),
            jax.ShapeDtypeStruct((share, heads), F32),
            jax.ShapeDtypeStruct((piece, kvw), F32),
            jax.ShapeDtypeStruct((piece, kvw), F32),
        ),
        in_specs=[VMEM_SPEC] * 5,
        out_specs=[VMEM_SPEC] * 7,
        scratch_shapes=scatter_four_scratch(rows, width)
        + scatter_four_scratch(rows, width)
        + scatter_line_scratch(chips, *weight_part.shape[2:])
        + [
            pltpu.SemaphoreType.DMA,
            pltpu.SemaphoreType.DMA,
            pltpu.VMEM((share, kvw), F32),
            pltpu.VMEM((section, piece, kvw), F32),
            pltpu.SemaphoreType.DMA((section,)),
            pltpu.SemaphoreType.DMA((section,)),
            pltpu.SemaphoreType.DMA,
        ],
        compiler_params=pltpu.CompilerParams(
            collective_id=4, has_side_effects=True, vmem_limit_bytes=VMEM_LIMIT
        ),
        name="reduce_last",
    )(rows_part, source_part, weight_part, hout, cot)


def on_device(
    tp, seq, section, h_in, memory, cotangent, block_docs, w_query, w_out, self_weight, cache_weight
):
    is_self = lax.axis_index("section") == 0
    hidden, cot = h_in[0], cotangent[0]
    source = jnp.where(is_self, hidden, memory[0])
    wq, wo = w_query[0], w_out[0]
    width = wq.shape[0]
    self_w = self_weight.reshape(width, -1)
    cache_w = cache_weight.reshape(width, -1)
    full_s, full_h, full_c = gather_rows(tp, source, hidden, cot)
    q, kv, payload, dout, rh, rs = project(
        tp, block_docs, full_h, full_s, full_c, wq, wo, self_w, cache_w
    )
    all_kv = gather_keys(seq, payload)
    attn, proj, gq, dot, dkv = attend(block_docs, q, dout, all_kv, wo)
    hout, sums = reduce_first(tp, seq, proj, hidden, dkv)
    rows_part, source_part, weight_part = backward(
        tp, full_h, full_s, full_c, wq, self_w, cache_w, gq, dot, attn, kv, sums, rh, rs
    )
    passed, gin, gmem, gwq, gwo, gself, gcache = reduce_last(
        tp, seq, section, rows_part, source_part, weight_part, hout, cot, wq.shape[1], self_w.shape[1]
    )
    kv_shape = (gself.shape[0],) + self_weight.shape[1:]
    return (
        passed[None], gin[None], gmem[None], gwq[None], gwo.T[None],
        gself.reshape(kv_shape), gcache.reshape(kv_shape),
    )


def solution(mesh):
    sizes = mesh.shape
    return jax.shard_map(
        functools.partial(on_device, sizes["tp"], sizes["seq"], sizes["section"]),
        mesh=mesh,
        in_specs=(
            P("section", "seq", "tp"),
            P("section", "seq", "tp"),
            P("section", "seq", "tp"),
            P("section", "seq"),
            P("section", None, "tp"),
            P("section", "tp", None),
            P(None, None, "tp"),
            P(None, None, "tp"),
        ),
        out_specs=(
            P("section", "seq", "tp"),
            P("section", "seq", "tp"),
            P("section", "seq", "tp"),
            P("section", "seq", "tp"),
            P("section", "tp", "seq"),
            P(("seq", "section"), None, "tp"),
            P(("seq", "section"), None, "tp"),
        ),
        check_vma=False,
    )
```

time: 667 us -> 230 us (0.34)
  waiting for transfers between devices: 421 us -> 0 us
  Pallas kernels: 0 us -> 215 us
  matrix products: 94.9 us -> 0 us
  local copies, waits for them, and re-layouts: 70.7 us -> 12.7 us
  other arithmetic: 35.1 us -> 1.9 us
  blocking collectives: 24 us -> 0 us
  between operations: 15.2 us -> 0.7 us
    reduce_scatter x6 -> x0, waiting for transfers between devices: 312 us -> none  [the longest x1 149 us: on_device(): lax.psum_scatter(jnp.stack([jnp.where(self_section, product, 0.0), jnp.wh...]
    pallas_call x0 -> x7, Pallas kernels: none -> 215 us  [the longest x1 80.2 us: reduce_last(): pl.pallas_call(functools.partial(reduce_last_kernel, tp, seq, section), o...]
    all_gather x4 -> x0, waiting for transfers between devices: 97.3 us -> none  [the longest x1 39.8 us: on_device(): lax.all_gather(packed, 'seq', axis=0, tiled=True)]
    dot_general x65 -> x0, matrix products: 94.9 us -> none  [the longest x16 23 us: block_scores(): jnp.einsum('tgjd,ugd->tgju', query_unit, key_block, preferred_element_typ...]
    unnamed x1 -> x0, blocking collectives: 13.9 us -> none
    dynamic_slice x16 -> x0, local copies, waits for them, and re-layouts: 11.9 us -> none  [on_device(): lax.scan(forward_step, (start_num, start_den), (key_all, value_all, key_p...]
    eq x16 -> x0, local copies, waits for them, and re-layouts: 11.6 us -> none  [visible(): same_doc = query_doc[:, None] == key_doc[None, :]]
    unnamed x73 -> x11, local copies, waits for them, and re-layouts: 17.2 us -> 5.72 us
  transfers between devices with their start and end apart: 11 -> 0, of which waited for: 11 -> 0; matrix products, arithmetic and copies ran while one was open for 8% -> 0% of each run, Pallas kernels for 0% -> 0%
where the time goes in v1:
time: 230 us
  Pallas kernels  215 us (93%)
  local copies, waits for them, and re-layouts  12.7 us (6%)
    pallas_call x1, Pallas kernels, reduce_last(): pl.pallas_call(functools.partial(reduce_last_kernel, tp, seq, section), o...  80.2 us
    pallas_call x1, Pallas kernels, gather_rows(): pl.pallas_call(functools.partial(gather_rows_kernel, count), out_shape=(f...  43.3 us
    pallas_call x1, Pallas kernels, reduce_first(): pl.pallas_call(functools.partial(reduce_first_kernel, tp, seq), out_shape...  39.5 us
    pallas_call x1, Pallas kernels, gather_keys(): pl.pallas_call(functools.partial(gather_keys_kernel, count), out_shape=ja...  26.1 us
    pallas_call x1, Pallas kernels, backward(): pl.pallas_call(backward_kernel, grid=(steps,), out_shape=(jax.ShapeDtypeS...  10.4 us
    pallas_call x1, Pallas kernels, project(): pl.pallas_call(project_kernel, grid=(steps,), out_shape=(jax.ShapeDtypeSt...  7.56 us
    pallas_call x1, Pallas kernels, attend(): pl.pallas_call(attend_kernel, out_shape=(jax.ShapeDtypeStruct((rows, cols...  7.45 us
    unnamed x11, local copies, waits for them, and re-layouts  5.72 us

profile of v1, /device:TPU:2, one launch (start us, length us, event | category | flops | bytes accessed | tf_op | source)
XLA Modules:
  0.0 229.8 jit_solution(3049180660930374844)
XLA Ops:
  0.6 1.9 bitcast_select_fusion.src_ref
  2.5 4.0 %copy_bitcast_fusion = (bf16[3072,256]{1,0:T(8,128)(2,1)}, bf16[3072,256]{1,0:T(8,128)(2,1)}) fusion(bf16[384,8,2,128]{3,2,1,0:T(2,128)(2,1)} %bitcast.32, bf16[384,8,2,128]{3,2,1,0:T(2,128)(2,1)} %bitcast.33), kind=kLoop, calls=%fused_computation | loop fusion | bytes 6291456 | tf_op jit(solution)/shard_map/reshape | solution.py:802
  6.5 43.3 %gather_rows.1 = (bf16[256,3072]{1,0:T(8,128)(2,1)}, bf16[256,3072]{1,0:T(8,128)(2,1)}, bf16[256,3072]{1,0:T(8,128)(2,1)}) custom-call(bf16[256,768]{1,0:T(8,128)(2,1)} %bitcast_select_fusion.src_ref, bf16[256,768]{1,0:T(8,128)(2,1)} %bitcast.27, bf16[256,768]{1,0:T(8,128)(2,1)} %bitcast.30), custom_call_target="tpu_custom_call" | custom-call | tf_op jit(solution)/shard_map/gather_rows/pallas_call | solution.py:156
  49.9 7.6 %project.1 = (f32[256,384]{1,0:T(8,128)}, f32[256,256]{1,0:T(8,128)}, bf16[272,256]{1,0:T(8,128)(2,1)}, bf16[256,384]{1,0:T(8,128)(2,1)}, f32[256,128]{1,0:T(8,128)}, /*index=5*/f32[256,128]{1,0:T(8,128)}) custom-call(s32[1,2]{1,0:T(1,128)} %docs_ref.3, bf16[256,3072]{1,0:T(8,128)(2,1)} %get-tuple-element.33.h_ref, ...), custom_call_target="tpu_custom_call" | custom-call | tf_op jit(solution)/shard_map/project/pallas_call | solution.py:227
  57.4 26.1 %gather_keys.1.kv_ref = bf16[16,272,256]{2,1,0:T(8,128)(2,1)} custom-call(bf16[272,256]{1,0:T(8,128)(2,1)} %get-tuple-element.38.in_ref), custom_call_target="tpu_custom_call" | custom-call | tf_op jit(solution)/shard_map/gather_keys/pallas_call | solution.py:311
  83.6 7.4 %attend.1 = (bf16[256,384]{1,0:T(8,128)(2,1)}, bf16[256,3072]{1,0:T(8,128)(2,1)}, bf16[256,384]{1,0:T(8,128)(2,1)}, f32[256,128]{1,0:T(8,128)}, bf16[16,256,256]{2,1,0:T(8,128)(2,1)}) custom-call(s32[1,2]{1,0:T(1,128)} %docs_ref.3, f32[256,384]{1,0:T(8,128)} %get-tuple-element.36.q_ref, bf16[256,384]{1,0:T(8,128)(2,1)} %get-tuple-element.37.dout_ref, ...), custom_call_target="tpu_custom_call" | custom-call | tf_op jit(solution)/shard_map/attend/pallas_call | solution.py:433
  91.0 39.5 %reduce_first.1 = (bf16[256,768]{1,0:T(8,128)(2,1)}, f32[256,256]{1,0:T(8,128)}) custom-call(bf16[256,3072]{1,0:T(8,128)(2,1)} %get-tuple-element.43.proj_ref, bf16[256,768]{1,0:T(8,128)(2,1)} %bitcast.28, bf16[8,2,256,256]{3,2,1,0:T(8,128)(2,1)} %bitcast.29), custom_call_target="tpu_custom_call" | custom-call | tf_op jit(solution)/shard_map/reduce_first/pallas_call | solution.py:605
  130.5 10.4 %backward.1 = (bf16[256,3072]{1,0:T(8,128)(2,1)}, bf16[256,3072]{1,0:T(8,128)(2,1)}, bf16[3072,1024]{1,0:T(8,128)(2,1)}) custom-call(bf16[256,3072]{1,0:T(8,128)(2,1)} %get-tuple-element.33.h_ref, bf16[256,3072]{1,0:T(8,128)(2,1)} %get-tuple-element.34.src_ref, bf16[256,3072]{1,0:T(8,128)(2,1)} %get-tuple-element.35.cot_ref, bf16[3072,384]{1,0:T(8,128)(2,1)} %bitcast.25, ...), custom_call_target="tpu_custom_call" | custom-call | tf_op jit(solution)/shard_map/backward/pallas_call | solution.py:664
  140.9 80.2 %reduce_last.1 = (bf16[256,768]{1,0:T(8,128)(2,1)}, bf16[256,768]{1,0:T(8,128)(2,1)}, bf16[256,768]{1,0:T(8,128)(2,1)}, f32[192,384]{1,0:T(8,128)}, f32[192,384]...) custom-call(bf16[256,3072]{1,0:T(8,128)(2,1)} %get-tuple-element.48.rows_ref, ...), custom_call_target="tpu_custom_call" | custom-call | tf_op jit(solution)/shard_map/reduce_last/pallas_call | solution.py:761
  221.1 0.0 copy-start
  221.1 0.0 copy-start.2
  221.1 0.0 copy-start.1
  221.1 1.5 reshape.36
  222.6 1.4 reshape.37
  224.1 1.8 copy.24
  225.8 1.8 copy.25
  227.6 0.0 copy-done
  227.6 0.7 copy.26
  228.4 0.0 copy-done.2
  228.4 0.7 copy.27
  229.1 0.0 copy-done.1
  229.1 0.7 copy.28
Async XLA Ops:
  221.1 6.5 %copy-start = (bf16[256,768]{1,0:T(8,128)(2,1)S(1)}, bf16[256,768]{1,0:T(8,128)(2,1)}, u32[]{:S(2)}) copy-start(bf16[256,768]{1,0:T(8,128)(2,1)} %get-tuple-element.54) | copy-start | bytes 1179652
  221.1 7.3 %copy-start.2 = (f32[192,384]{1,0:T(8,128)S(1)}, f32[192,384]{1,0:T(8,128)}, u32[]{:S(2)}) copy-start(f32[192,384]{1,0:T(8,128)} %get-tuple-element.55) | copy-start | bytes 884740
  221.1 8.0 %copy-start.1 = (f32[192,384]{1,0:T(8,128)S(1)}, f32[192,384]{1,0:T(8,128)}, u32[]{:S(2)}) copy-start(f32[192,384]{1,0:T(8,128)} %get-tuple-element.56) | copy-start | bytes 884740

commit v2 on v0

v2 whole, which is shorter than its diff:
```python
import functools
import math

import jax
import jax.numpy as jnp
from jax import lax
from jax.experimental import pallas as pl
from jax.experimental.pallas import tpu as pltpu
from jax.sharding import PartitionSpec as P

MESH = pl.DeviceIdType.MESH
HEAD_DIM = 128
BLK = 128
WIN = 1024
SCALE = 40.0
EPS = 1e-06
EXP2_SCALE = SCALE * math.log2(math.e)
F32 = jnp.float32
BF16 = jnp.bfloat16
DOC_ROWS = 16
VMEM_SPEC = pl.BlockSpec(memory_space=pltpu.VMEM)
ANY_SPEC = pl.BlockSpec(memory_space=pl.ANY)
SMEM_SPEC = pl.BlockSpec(memory_space=pltpu.SMEM)
VMEM_LIMIT = 60 * 1024 * 1024


def nt(left, right):
    return lax.dot_general(left, right, (((1,), (1,)), ((), ())), preferred_element_type=F32)


def nn(left, right):
    return lax.dot_general(left, right, (((1,), (0,)), ((), ())), preferred_element_type=F32)


def tn(left, right):
    return lax.dot_general(left, right, (((0,), (0,)), ((), ())), preferred_element_type=F32)


def remote(src, dst, send_sem, recv_sem, device):
    return pltpu.make_async_remote_copy(
        src_ref=src,
        dst_ref=dst,
        send_sem=send_sem,
        recv_sem=recv_sem,
        device_id=device,
        device_id_type=MESH,
    )


def greet(devices):
    barrier = pltpu.get_barrier_semaphore()
    for device in devices:
        pl.semaphore_signal(barrier, inc=1, device_id=device, device_id_type=MESH)
    pl.semaphore_wait(barrier, len(devices))


def run_together(*streams):
    live = list(streams)
    while live:
        for stream in list(live):
            try:
                next(stream)
            except StopIteration:
                live.remove(stream)


class Ring:
    def __init__(self, axis, count):
        self.axis = axis
        self.me = lax.axis_index(axis)
        self.count = count

    def at(self, step):
        return lax.rem(self.me + step + self.count, self.count)

    def device(self, step):
        return {self.axis: self.at(step)}


class Line:
    def __init__(self, count):
        self.me = lax.axis_index("seq")
        self.chips = count // 2
        self.chip = self.me // 2
        self.core = self.me - self.chip * 2
        self.other = 1 - self.core

    def chip_at(self, step):
        return lax.rem(self.chip + step + self.chips, self.chips)

    def index(self, step):
        return self.chip_at(step) * 2 + self.core

    def device(self, step):
        return {"seq": self.index(step)}

    def partner(self):
        return {"seq": self.chip * 2 + self.other}


def gather_four(ring, full, send, recv):
    rows = full.shape[0]
    width = full.shape[1] // ring.count
    lo, hi = pl.ds(0, rows // 2), pl.ds(rows // 2, rows // 2)

    def block(half, step):
        return full.at[half, pl.ds(pl.multiple_of(ring.at(step) * width, 128), width)]

    def move(piece, slot, step):
        copy = remote(piece, piece, send.at[slot], recv.at[slot], ring.device(step))
        copy.start()
        return copy

    right_lo, left_hi = move(block(lo, 0), 0, 1), move(block(hi, 0), 1, -1)
    right_hi, left_lo = move(block(hi, 0), 2, 1), move(block(lo, 0), 3, -1)
    yield
    right_lo.wait_recv()
    relay_right = move(block(lo, -1), 4, 1)
    left_hi.wait_recv()
    relay_left = move(block(hi, 1), 5, -1)
    yield
    for copy in (right_hi, left_lo, relay_right, relay_left):
        copy.wait_recv()
    yield
    for copy in (right_lo, left_hi, right_hi, left_lo, relay_right, relay_left):
        copy.wait_send()


def gather_line(line, full, send, recv, to_core, from_core):
    rows = full.shape[1]
    cut = (rows // 2 + 15) // 16 * 16
    halves = {1: pl.ds(0, cut), -1: pl.ds(cut, rows - cut)}
    copies, hops, passed = [], {}, []

    def move(piece, s, r, device):
        copy = remote(piece, piece, s, r, device)
        copy.start()
        copies.append(copy)
        return copy

    last = line.chips // 2
    own = full.at[line.me]
    for way, d in ((0, 1), (1, -1)):
        hops[way] = move(own, send.at[way, 0], recv.at[way, 0], line.device(d))
    passed.append(move(own, to_core.at[0], from_core.at[0], line.partner()))
    yield
    slot = 1
    for hop in range(1, last + 1):
        for way, d in ((0, 1), (1, -1)):
            hops[way].wait_recv()
            block = line.index(-d * hop)
            piece = full.at[block]
            if hop < last:
                ahead = piece if hop < last - 1 else full.at[block, halves[d], :]
                hops[way] = move(ahead, send.at[way, hop], recv.at[way, hop], line.device(d))
            else:
                piece = full.at[block, halves[d], :]
            passed.append(move(piece, to_core.at[slot], from_core.at[slot], line.partner()))
            slot += 1
        yield
    for copy in passed:
        copy.wait_recv()
    yield
    for copy in copies:
        copy.wait_send()


def gather_line_scratch(chips):
    last = chips // 2
    return [
        pltpu.SemaphoreType.DMA((2, last)),
        pltpu.SemaphoreType.DMA((2, last)),
        pltpu.SemaphoreType.DMA((2 * last + 1,)),
        pltpu.SemaphoreType.DMA((2 * last + 1,)),
    ]


def scatter_four(ring, in_ref, buf, stage, send, recv, finish):
    rows = in_ref.shape[0]
    width = in_ref.shape[1] // ring.count
    lo, hi = pl.ds(0, rows // 2), pl.ds(rows // 2, rows // 2)

    def block(half, step):
        return in_ref.at[half, pl.ds(pl.multiple_of(ring.at(step) * width, 128), width)]

    def move(src, slot, step):
        copy = remote(src, buf.at[slot], send.at[slot], recv.at[slot], ring.device(step))
        copy.start()
        return copy

    copies = [
        move(block(lo, 2), 0, 1),
        move(block(hi, 2), 1, -1),
        move(block(hi, 1), 2, 1),
        move(block(lo, -1), 3, -1),
    ]
    yield
    copies[0].wait_recv()
    stage[0] = (buf[0].astype(F32) + block(lo, 1)[...].astype(F32)).astype(BF16)
    copies.append(move(stage.at[0], 4, 1))
    yield
    copies[1].wait_recv()
    stage[1] = (buf[1].astype(F32) + block(hi, -1)[...].astype(F32)).astype(BF16)
    copies.append(move(stage.at[1], 5, -1))
    yield
    copies[2].wait_recv()
    copies[5].wait_recv()
    finish(hi, block(hi, 0)[...].astype(F32) + buf[2].astype(F32) + buf[5].astype(F32))
    yield
    copies[3].wait_recv()
    copies[4].wait_recv()
    finish(lo, block(lo, 0)[...].astype(F32) + buf[3].astype(F32) + buf[4].astype(F32))
    yield
    for copy in copies:
        copy.wait_send()


def scatter_four_scratch(rows, width):
    return [
        pltpu.VMEM((6, rows // 2, width), BF16),
        pltpu.VMEM((2, rows // 2, width), BF16),
        pltpu.SemaphoreType.DMA((6,)),
        pltpu.SemaphoreType.DMA((6,)),
    ]


def scatter_line(line, in_ref, other, buf, stage, send, recv, to_core, from_core, finish):
    rows = in_ref.shape[1]
    last = line.chips // 2
    halves = (pl.ds(0, rows // 2), pl.ds(rows // 2, rows // 2))
    order = [last]
    for k in range(last - 1, 0, -1):
        order += [k, -k]
    order.append(0)
    pieces = {}
    copies = []
    for slot, step in enumerate(order):
        chip = line.chip_at(step)
        copy = remote(
            in_ref.at[chip * 2 + line.other], other.at[chip], to_core.at[slot], from_core.at[slot], line.partner()
        )
        copy.start()
        copies.append(copy)
        pieces[step] = copy
    yield
    ready = set()

    def own(step, half):
        if abs(step) == last:
            step = last
        if step not in ready:
            pieces[step].wait_recv()
            ready.add(step)
        chip = line.chip_at(step)
        return in_ref[chip * 2 + line.core, half, :].astype(F32) + other[chip, half, :].astype(F32)

    sent = {}
    plan = [(last, 0)]
    for k in range(last - 1, 0, -1):
        plan += [(k, 1), (k, 0)]
    for k, which in plan:
        for way, d in ((0, 1), (1, -1)):
            part = which if way == 0 else 1 - which
            half = halves[part]
            value = own(d * k, half)
            if (way, k + 1, part) in sent:
                sent[way, k + 1, part].wait_recv()
                value = value + buf[way, k, half, :].astype(F32)
            stage[way, k - 1, half, :] = value.astype(BF16)
            copy = remote(
                stage.at[way, k - 1, half, :],
                buf.at[way, k - 1, half, :],
                send.at[way, k - 1, part],
                recv.at[way, k - 1, part],
                line.device(d),
            )
            copy.start()
            sent[way, k, part] = copy
            copies.append(copy)
            yield
    for part in (1, 0):
        half = halves[part]
        value = own(0, half)
        for way in (0, 1):
            sent[way, 1, part].wait_recv()
            value = value + buf[way, 0, half, :].astype(F32)
        finish(half, value)
        yield
    for copy in copies:
        copy.wait_send()


def scatter_line_scratch(chips, rows, width):
    last = chips // 2
    return [
        pltpu.VMEM((chips, rows, width), BF16),
        pltpu.VMEM((2, last, rows, width), BF16),
        pltpu.VMEM((2, last, rows, width), BF16),
        pltpu.SemaphoreType.DMA((2, last, 2)),
        pltpu.SemaphoreType.DMA((2, last, 2)),
        pltpu.SemaphoreType.DMA((chips,)),
        pltpu.SemaphoreType.DMA((chips,)),
    ]


def step_kernel(
    tp, seq, section,
    docs_ref, h_ref, mem_ref, cot_ref, wq_any, wo_any, kvw_any,
    passed_ref, gin_ref, gmem_ref, gwq_ref, gwo_ref, gself_ref, gcache_ref,
    full_h, full_s, full_c, wq, wo, kvw,
    q_raw, kv_raw, all_kv, q_unit, dout, weights, acc, dq, attn, gq, gkv, hout,
    proj, rows_part, source_part, dkv, part_q, part_o, part_kv, sums, mine, got,
    load, gather_send, gather_recv, pass_send, pass_recv, ex_send, ex_recv, ex_local,
    *scratch,
):
    line_gather, scratch = scratch[:4], scratch[4:]
    four = [scratch[4 * k : 4 * k + 4] for k in range(3)]
    scratch = scratch[12:]
    lines = [scratch[7 * k : 7 * k + 7] for k in range(4)]
    ring, line, sections = Ring("tp", tp), Line(seq), Ring("section", section)
    me = line.me
    is_self = sections.me == 0
    rows, width = h_ref.shape
    model = width * tp
    heads = wq.shape[1] // HEAD_DIM
    chunks = seq

    def cols(step):
        return pl.ds(pl.multiple_of(ring.at(step) * width, 128), width)

    own_h = pltpu.make_async_copy(h_ref, full_h.at[:, cols(0)], load.at[0])
    own_c = pltpu.make_async_copy(cot_ref, full_c.at[:, cols(0)], load.at[1])
    source_self = pltpu.make_async_copy(h_ref, full_s.at[:, cols(0)], load.at[2])
    source_cross = pltpu.make_async_copy(mem_ref, full_s.at[:, cols(0)], load.at[2])

    @pl.when(is_self)
    def _():
        source_self.start()

    @pl.when(jnp.logical_not(is_self))
    def _():
        source_cross.start()

    own_h.start()
    own_c.start()
    load_kvw = pltpu.make_async_copy(kvw_any, kvw, load.at[3])
    load_wq = pltpu.make_async_copy(wq_any, wq, load.at[4])
    load_wo = pltpu.make_async_copy(wo_any, wo, load.at[5])
    load_kvw.start()
    load_wq.start()
    load_wo.start()
    greet(
        [ring.device(1), ring.device(-1), line.device(1), line.device(-1), line.partner()]
        + [sections.device(k) for k in range(1, section)]
    )
    gather_s, gather_h, gather_c = [
        gather_four(ring, full, gather_send.at[k], gather_recv.at[k])
        for k, full in enumerate((full_s, full_h, full_c))
    ]
    keys = gather_line(line, all_kv, *line_gather)
    blocks = [pl.ds(k * width, width) for k in range(tp)]

    def factor(full):
        total = jnp.zeros((rows, 128), F32)
        for span in blocks:
            wide = full[:, span].astype(F32)
            wide = wide * wide
            for first in range(0, width, 128):
                total += wide[:, first : first + 128]
        return lax.rsqrt(jnp.sum(total, axis=1, keepdims=True) / model + EPS)

    def head_rows(head):
        return pl.ds(head * rows, rows)

    def head_cols(head):
        return pl.ds(head * HEAD_DIM, HEAD_DIM)

    source_self.wait()
    next(gather_s)
    own_h.wait()
    own_c.wait()
    acc[...] = jnp.zeros_like(acc)
    dq[...] = jnp.zeros_like(dq)
    low = jnp.where(is_self, jnp.maximum(me - WIN // rows, 0), 0)
    zero_chunk = jnp.zeros((rows, 2 * HEAD_DIM), BF16)

    @pl.loop(0, low)
    def _(j):
        dkv[j] = zero_chunk

    @pl.loop(me + 1, chunks)
    def _(j):
        dkv[j] = zero_chunk

    load_kvw.wait()
    next(gather_s)
    next(gather_h)
    next(gather_s)
    rs = factor(full_s)
    kv = nn(full_s[:, blocks[0]], kvw[blocks[0], :])
    for span in blocks[1:]:
        kv += nn(full_s[:, span], kvw[span, :])
    kv = kv * rs
    kv_raw[...] = kv
    key, value = kv[:, :HEAD_DIM], kv[:, HEAD_DIM:]
    unit = key * lax.rsqrt(jnp.sum(key * key, axis=1, keepdims=True) + EPS)
    all_kv[me, 0:rows, 0:HEAD_DIM] = unit.astype(BF16)
    all_kv[me, 0:rows, HEAD_DIM:] = value.astype(BF16)
    doc_lane = lax.broadcasted_iota(jnp.int32, (DOC_ROWS, 2 * BLK), 1)
    docs = jnp.where(doc_lane < BLK, docs_ref[0, 0], docs_ref[0, 1])
    all_kv[me, rows:, :] = docs.astype(F32).astype(BF16)
    next(keys)
    next(gather_h)
    next(gather_c)
    load_wq.wait()
    next(keys)
    next(keys)
    next(gather_h)
    rh = factor(full_h)
    q = nn(full_h[:, blocks[0]], wq[blocks[0], :])
    for span in blocks[1:]:
        q += nn(full_h[:, span], wq[span, :])
    q_raw[...] = q * rh
    for head in range(heads):
        part = q_raw[:, head_cols(head)]
        unit = part * lax.rsqrt(jnp.sum(part * part, axis=1, keepdims=True) + EPS)
        q_unit[head_rows(head), :] = unit.astype(BF16)
    next(keys)
    next(gather_c)
    next(keys)
    next(keys)

    row = lax.broadcasted_iota(jnp.int32, (rows, 1), 0)
    lane = lax.broadcasted_iota(jnp.int32, (1, rows), 1)
    query_doc = jnp.where(row < BLK, docs_ref[0, 0], docs_ref[0, 1]).astype(F32)
    query_pos = me * rows + row
    upper = jnp.where(is_self, query_pos, query_pos // BLK * BLK + BLK - 1)
    lower = jnp.where(is_self, query_pos - WIN, -1)
    ones = jnp.ones((rows, HEAD_DIM), BF16)

    @pl.loop(low, me + 1)
    def _(j):
        key = all_kv[j, 0:rows, 0:HEAD_DIM]
        value = jnp.concatenate([all_kv[j, 0:rows, HEAD_DIM:], ones], axis=1)
        key_doc = all_kv[j, rows:, :].astype(F32)[0:1, :]
        key_pos = j * rows + lane
        seen = (key_doc == query_doc) & (key_pos <= upper) & (key_pos > lower)
        for head in range(heads):
            score = nt(q_unit[head_rows(head), :], key)
            weight = jnp.where(seen, jnp.exp2(score * EXP2_SCALE), 0.0).astype(BF16)
            weights[j, head_rows(head), :] = weight
            acc[head_rows(head), :] += nn(weight, value)

    for head in range(heads):
        total = acc[head_rows(head), :]
        attn[:, head_cols(head)] = (total[:, :HEAD_DIM] * (1.0 / total[:, HEAD_DIM:])).astype(BF16)
    load_wo.wait()
    attn_now = attn[...]
    for span in blocks:
        proj[:, span] = nn(attn_now, wo[:, span]).astype(BF16)

    def finish_rows(half, value):
        hout[half, :] = (full_h[half, cols(0)].astype(F32) + value).astype(BF16)

    def finish_input(half, value):
        gin_ref[half, :] = (full_c[half, cols(0)].astype(F32) + value).astype(BF16)

    def finish_memory(half, value):
        gmem_ref[half, :] = value.astype(BF16)

    def finish_keys(half, value):
        sums[half, :] = value

    def finish_wq(half, value):
        gwq_ref[half, :] = value

    def finish_wo(half, value):
        gwo_ref[half, :] = value

    def finish_kv(half, value):
        mine[half, :] = value

    red_hout = scatter_four(ring, proj, *four[0], finish_rows)
    next(red_hout)
    next(gather_c)
    grad = nt(full_c[:, blocks[0]], wo[:, blocks[0]])
    for span in blocks[1:]:
        grad += nt(full_c[:, span], wo[:, span])
    share = part_o.shape[1]
    per_block = width // share
    for k, span in enumerate(blocks):
        value = tn(full_c[:, span], attn_now).astype(BF16)
        part_o[k * per_block : (k + 1) * per_block] = value.reshape(per_block, share, value.shape[1])
    red_wo = scatter_line(line, part_o, *lines[0], finish_wo)
    next(red_wo)
    deltas = []
    for head in range(heads):
        inverse = 1.0 / acc[head_rows(head), HEAD_DIM:]
        part = grad[:, head * HEAD_DIM : (head + 1) * HEAD_DIM].astype(BF16).astype(F32)
        delta = jnp.sum(part * attn[:, head_cols(head)].astype(F32), axis=1, keepdims=True)
        dout[head_rows(head), :] = (part * inverse).astype(BF16)
        deltas.append(delta * inverse[:, 0:1])

    def advance(stream, times):
        for _ in range(times):
            next(stream, None)

    def back(start, stop):
        @pl.loop(jnp.maximum(low, start), jnp.minimum(me + 1, stop))
        def _(j):
            key = all_kv[j, 0:rows, 0:HEAD_DIM]
            value = all_kv[j, 0:rows, HEAD_DIM:]
            grad_key = jnp.zeros((rows, HEAD_DIM), F32)
            grad_value = jnp.zeros((rows, HEAD_DIM), F32)
            for head in range(heads):
                weight = weights[j, head_rows(head), :]
                part = dout[head_rows(head), :]
                grad_prob = nt(part, value)
                grad_score = (weight.astype(F32) * (grad_prob - deltas[head])).astype(BF16)
                dq[head_rows(head), :] += nn(grad_score, key)
                grad_key += tn(grad_score, q_unit[head_rows(head), :])
                grad_value += tn(weight, part)
            dkv[j, :, 0:HEAD_DIM] = (SCALE * grad_key).astype(BF16)
            dkv[j, :, HEAD_DIM:] = grad_value.astype(BF16)

    quarter = chunks // 4
    for k in range(4):
        back(k * quarter, (k + 1) * quarter)
        if k < 3:
            advance(red_hout, 2)
            advance(red_wo, 4)
    red_keys = scatter_line(line, dkv, *lines[1], finish_keys)
    next(red_keys)
    pass_on = pass_along(sections, hout, passed_ref, pass_send, pass_recv)
    next(pass_on)

    total = jnp.zeros((rows, 1), F32)
    scaled = []
    for head in range(heads):
        part = q_raw[:, head_cols(head)]
        slope = SCALE * dq[head_rows(head), :]
        inverse = lax.rsqrt(jnp.sum(part * part, axis=1, keepdims=True) + EPS)
        along = jnp.sum(part * slope, axis=1, keepdims=True)
        value = (inverse * slope - part * (inverse * inverse * inverse * along)).astype(BF16)
        gq[:, head_cols(head)] = value
        total += jnp.sum(value.astype(F32) * part, axis=1, keepdims=True)
        scaled.append((value.astype(F32) * rh).astype(BF16))
    scaled_q = jnp.concatenate(scaled, axis=1)
    fix = rh * rh * total / model
    for span in blocks:
        value = nt(gq[...], wq[span, :]) * rh - full_h[:, span].astype(F32) * fix
        rows_part[:, span] = value.astype(BF16)
    red_rows = scatter_four(ring, rows_part, *four[1], finish_input)
    next(red_rows)
    advance(red_keys, 4)
    for k, span in enumerate(blocks):
        value = tn(full_h[:, span], scaled_q).astype(BF16)
        part_q[k * per_block : (k + 1) * per_block] = value.reshape(per_block, share, value.shape[1])
        advance(red_keys, 1)
    red_wq = scatter_line(line, part_q, *lines[2], finish_wq)
    while next(red_keys, 1) is None:
        next(red_rows, None)
        next(red_wo, None)
    next(red_wq)
    summed = sums[...]
    kv = kv_raw[...]
    key, slope = kv[:, :HEAD_DIM], summed[:, :HEAD_DIM]
    inverse = lax.rsqrt(jnp.sum(key * key, axis=1, keepdims=True) + EPS)
    along = jnp.sum(key * slope, axis=1, keepdims=True)
    slope = inverse * slope - key * (inverse * inverse * inverse * along)
    both = jnp.concatenate([slope, summed[:, HEAD_DIM:]], axis=1).astype(BF16)
    total = jnp.sum(both.astype(F32) * kv, axis=1, keepdims=True)
    fix = rs * rs * total / model
    for span in blocks:
        value = nt(both, kvw[span, :]) * rs - full_s[:, span].astype(F32) * fix
        source_part[:, span] = value.astype(BF16)
    red_source = scatter_four(ring, source_part, *four[2], finish_memory)
    next(red_source)
    scaled_kv = (both.astype(F32) * rs).astype(BF16)
    for k, span in enumerate(blocks):
        value = tn(full_s[:, span], scaled_kv).astype(BF16)
        part_kv[k * per_block : (k + 1) * per_block] = value.reshape(per_block, share, value.shape[1])
        next(red_wo, None)
        next(red_wq, None)
    red_kv = scatter_line(line, part_kv, *lines[3], finish_kv)
    run_together(red_kv, red_wq, red_source, red_rows, red_wo)

    piece = gself_ref.shape[0]
    copies = []
    for k in range(1, section):
        first = pl.multiple_of(sections.at(k) * piece, 8)
        copy = remote(
            mine.at[pl.ds(first, piece), :], got.at[sections.me], ex_send.at[k], ex_recv.at[k], sections.device(k)
        )
        copy.start()
        copies.append(copy)
    first = pl.multiple_of(sections.me * piece, 8)
    local = pltpu.make_async_copy(mine.at[pl.ds(first, piece), :], got.at[sections.me], ex_local)
    local.start()
    run_together(pass_on, red_hout, gather_s, gather_h, gather_c, keys)
    for copy in copies:
        copy.wait_recv()
    local.wait()
    gself_ref[...] = got[0]
    total = got[1]
    for k in range(2, section):
        total = total + got[k]
    gcache_ref[...] = total
    for copy in copies:
        copy.wait_send()


def pass_along(ring, in_ref, out_ref, send, recv):
    copy = remote(in_ref, out_ref, send, recv, ring.device(1))
    copy.start()
    yield
    copy.wait()


def whole_step(tp, seq, section, docs, hidden, memory, cot, wq, wo, kvw):
    rows, width = hidden.shape
    model, cols = wq.shape
    heads = cols // HEAD_DIM
    kv = kvw.shape[1]
    chips = seq // 2
    share = model // seq
    piece = share // section
    small = jax.ShapeDtypeStruct((rows, width), BF16)
    vmem = pltpu.VMEM
    dma = pltpu.SemaphoreType.DMA
    scratch = [
        vmem((rows, model), BF16), vmem((rows, model), BF16), vmem((rows, model), BF16),
        vmem((model, cols), BF16), vmem((cols, model), BF16), vmem((model, kv), BF16),
        vmem((rows, cols), F32), vmem((rows, kv), F32),
        vmem((seq, rows + DOC_ROWS, kv), BF16),
        vmem((heads * rows, HEAD_DIM), BF16), vmem((heads * rows, HEAD_DIM), BF16),
        vmem((seq, heads * rows, rows), BF16),
        vmem((heads * rows, 2 * HEAD_DIM), F32), vmem((heads * rows, HEAD_DIM), F32),
        vmem((rows, cols), BF16), vmem((rows, cols), BF16), vmem((rows, kv), BF16), vmem((rows, width), BF16),
        vmem((rows, model), BF16), vmem((rows, model), BF16), vmem((rows, model), BF16),
        vmem((seq, rows, kv), BF16),
        vmem((seq, share, cols), BF16), vmem((seq, share, cols), BF16), vmem((seq, share, kv), BF16),
        vmem((rows, kv), F32), vmem((share, kv), F32), vmem((section, piece, kv), F32),
        dma((6,)), dma((3, 6)), dma((3, 6)), dma, dma, dma((section,)), dma((section,)), dma,
    ]
    scratch += gather_line_scratch(chips)
    for _ in range(3):
        scratch += scatter_four_scratch(rows, width)
    for shape in ((share, cols), (rows, kv), (share, cols), (share, kv)):
        scratch += scatter_line_scratch(chips, *shape)
    return pl.pallas_call(
        functools.partial(step_kernel, tp, seq, section),
        out_shape=(
            small, small, small,
            jax.ShapeDtypeStruct((share, cols), F32), jax.ShapeDtypeStruct((share, cols), F32),
            jax.ShapeDtypeStruct((piece, kv), F32), jax.ShapeDtypeStruct((piece, kv), F32),
        ),
        in_specs=[SMEM_SPEC] + [ANY_SPEC] * 6,
        out_specs=[VMEM_SPEC] * 7,
        scratch_shapes=scratch,
        compiler_params=pltpu.CompilerParams(
            collective_id=1, has_side_effects=True, vmem_limit_bytes=VMEM_LIMIT
        ),
        name="step",
    )(docs, hidden, memory, cot, wq, wo, kvw)


def finish_kernel(passed, gin, gmem, gwq, gwo, gself, gcache, *outs):
    for source, target in zip((passed, gin, gmem, gwq), outs[:4]):
        target[...] = source[...]
    outs[4][...] = gwo[...].T
    for source, target in ((gself, outs[5]), (gcache, outs[6])):
        half = source.shape[1] // 2
        target[:, 0, :] = source[:, :half]
        target[:, 1, :] = source[:, half:]


def finish(results):
    shapes = [jax.ShapeDtypeStruct(x.shape, x.dtype) for x in results[:4]]
    shapes.append(jax.ShapeDtypeStruct(results[4].shape[::-1], F32))
    for x in results[5:]:
        shapes.append(jax.ShapeDtypeStruct((x.shape[0], 2, x.shape[1] // 2), F32))
    return pl.pallas_call(
        finish_kernel,
        out_shape=tuple(shapes),
        in_specs=[VMEM_SPEC] * 7,
        out_specs=[VMEM_SPEC] * 7,
        name="finish",
    )(*results)


def on_device(
    tp, seq, section, h_in, memory, cotangent, block_docs, w_query, w_out, self_weight, cache_weight
):
    is_self = lax.axis_index("section") == 0
    width = w_query.shape[1]
    kvw = jnp.where(is_self, self_weight, cache_weight).reshape(width, -1)
    results = whole_step(
        tp, seq, section, block_docs, h_in[0], memory[0], cotangent[0], w_query[0], w_out[0], kvw
    )
    passed, gin, gmem, gwq, gwo, gself, gcache = finish(results)
    return (passed[None], gin[None], gmem[None], gwq[None], gwo[None], gself, gcache)


def solution(mesh):
    sizes = mesh.shape
    return jax.shard_map(
        functools.partial(on_device, sizes["tp"], sizes["seq"], sizes["section"]),
        mesh=mesh,
        in_specs=(
            P("section", "seq", "tp"),
            P("section", "seq", "tp"),
            P("section", "seq", "tp"),
            P("section", "seq"),
            P("section", None, "tp"),
            P("section", "tp", None),
            P(None, None, "tp"),
            P(None, None, "tp"),
        ),
        out_specs=(
            P("section", "seq", "tp"),
            P("section", "seq", "tp"),
            P("section", "seq", "tp"),
            P("section", "seq", "tp"),
            P("section", "tp", "seq"),
            P(("seq", "section"), None, "tp"),
            P(("seq", "section"), None, "tp"),
        ),
        check_vma=False,
    )
```

time: 667 us -> 146 us (0.22)
  waiting for transfers between devices: 421 us -> 0 us
  Pallas kernels: 0 us -> 139 us
  matrix products: 94.9 us -> 0 us
  local copies, waits for them, and re-layouts: 70.7 us -> 3.22 us
  other arithmetic: 35.1 us -> 1.58 us
  blocking collectives: 24 us -> 0 us
  between operations: 15.2 us -> 0.65 us
    reduce_scatter x6 -> x0, waiting for transfers between devices: 312 us -> none  [the longest x1 149 us: on_device(): lax.psum_scatter(jnp.stack([jnp.where(self_section, product, 0.0), jnp.wh...]
    pallas_call x0 -> x2, Pallas kernels: none -> 139 us  [the longest x1 136 us: whole_step(): pl.pallas_call(functools.partial(step_kernel, tp, seq, section), out_shap...]
    all_gather x4 -> x0, waiting for transfers between devices: 97.3 us -> none  [the longest x1 39.8 us: on_device(): lax.all_gather(packed, 'seq', axis=0, tiled=True)]
    dot_general x65 -> x0, matrix products: 94.9 us -> none  [the longest x16 23 us: block_scores(): jnp.einsum('tgjd,ugd->tgju', query_unit, key_block, preferred_element_typ...]
    unnamed x73 -> x2, local copies, waits for them, and re-layouts: 17.2 us -> 3.22 us
    unnamed x1 -> x0, blocking collectives: 13.9 us -> none
    dynamic_slice x16 -> x0, local copies, waits for them, and re-layouts: 11.9 us -> none  [on_device(): lax.scan(forward_step, (start_num, start_den), (key_all, value_all, key_p...]
    eq x16 -> x0, local copies, waits for them, and re-layouts: 11.6 us -> none  [visible(): same_doc = query_doc[:, None] == key_doc[None, :]]
  transfers between devices with their start and end apart: 11 -> 0, of which waited for: 11 -> 0; matrix products, arithmetic and copies ran while one was open for 8% -> 0% of each run, Pallas kernels for 0% -> 0%
where the time goes in v2:
time: 146 us; the launch traced here: 144 us
  Pallas kernels  139 us (95%)
  local copies, waits for them, and re-layouts  3.22 us (2%)
  other arithmetic  1.58 us (1%)
    pallas_call x1, Pallas kernels, whole_step(): pl.pallas_call(functools.partial(step_kernel, tp, seq, section), out_shap...  136 us
    unnamed x2, local copies, waits for them, and re-layouts  3.22 us

profile of v2, /device:TPU:2, one launch (start us, length us, event | category | flops | bytes accessed | tf_op | source)
XLA Modules:
  0.0 144.5 jit_solution(14663669903827073293)
XLA Ops:
  0.6 1.6 %broadcast_select_fusion = bf16[768,8,128]{2,1,0:T(8,128)(2,1)S(1)} fusion(bf16[768,8,128]{2,1,0:T(8,128)(2,1)} %bitcast.21, bf16[768,8,128]{2,1,0:T(8,128)(2,1)} %bitcast.22, pred[]{:T(512)S(6)} %eq.3), kind=kLoop, calls=%fused_computation | loop fusion | flops 786432 | bytes 4718593 | tf_op jit(solution)/shard_map/jit(_where)/select_n | solution.py:697
  2.2 1.4 copy.18
  3.6 136.2 %step.1 = (bf16[256,768]{1,0:T(8,128)(2,1)}, bf16[256,768]{1,0:T(8,128)(2,1)}, bf16[256,768]{1,0:T(8,128)(2,1)}, f32[192,384]{1,0:T(8,128)}, f32[192,384]{1,0:T(...) custom-call(s32[1,2]{1,0:T(1,128)} %docs_ref.1, bf16[256,768]{1,0:T(8,128)(2,1)} %bitcast.24, bf16[256,768]{1,0:T(8,128)(2,1)} %bitcast.25, ...), custom_call_target="tpu_custom_call" | custom-call | tf_op jit(solution)/shard_map/step/pallas_call | solution.py:651
  139.8 2.8 %finish.1 = (bf16[256,768]{1,0:T(8,128)(2,1)}, bf16[256,768]{1,0:T(8,128)(2,1)}, bf16[256,768]{1,0:T(8,128)(2,1)}, f32[192,384]{1,0:T(8,128)}, f32[384,192]{1,0:...) custom-call(bf16[256,768]{1,0:T(8,128)(2,1)} %get-tuple-element.21.passed, ...), custom_call_target="tpu_custom_call" | custom-call | tf_op jit(solution)/shard_map/finish/pallas_call | solution.py:683
  142.6 1.9 %copy.15 = f32[1,384,192]{1,2,0:T(8,128)} copy(f32[1,384,192]{2,1,0:T(8,128)} %bitcast.23) | data formatting | bytes 589824

commit v3 on v2

--- a/solution.py
+++ b/solution.py
@@ -146,6 +146,7 @@
     yield
     slot = 1
     for hop in range(1, last + 1):
+        earlier, passed = passed, []
         for way, d in ((0, 1), (1, -1)):
             hops[way].wait_recv()
             block = line.index(-d * hop)
@@ -157,6 +158,8 @@
                 piece = full.at[block, halves[d], :]
             passed.append(move(piece, to_core.at[slot], from_core.at[slot], line.partner()))
             slot += 1
+        for copy in earlier:
+            copy.wait_recv()
         yield
     for copy in passed:
         copy.wait_recv()
@@ -224,26 +227,23 @@
     ]
 
 
-def scatter_line(line, in_ref, other, buf, stage, send, recv, to_core, from_core, finish):
+def scatter_line(line, in_ref, other, buf, stage, send, recv, to_core, from_core, finish, paced=False):
     rows = in_ref.shape[1]
     last = line.chips // 2
     halves = (pl.ds(0, rows // 2), pl.ds(rows // 2, rows // 2))
-    order = [last]
-    for k in range(last - 1, 0, -1):
-        order += [k, -k]
-    order.append(0)
-    pieces = {}
-    copies = []
-    for slot, step in enumerate(order):
-        chip = line.chip_at(step)
-        copy = remote(
-            in_ref.at[chip * 2 + line.other], other.at[chip], to_core.at[slot], from_core.at[slot], line.partner()
-        )
-        copy.start()
-        copies.append(copy)
-        pieces[step] = copy
-    yield
-    ready = set()
+    groups = [[last]] + [[k, -k] for k in range(last - 1, 0, -1)] + [[0]]
+    pieces, copies, ready, sent = {}, [], set(), {}
+
+    def offer(group):
+        for step in group:
+            slot = len(pieces)
+            chip = line.chip_at(step)
+            copy = remote(
+                in_ref.at[chip * 2 + line.other], other.at[chip], to_core.at[slot], from_core.at[slot], line.partner()
+            )
+            copy.start()
+            copies.append(copy)
+            pieces[step] = copy
 
     def own(step, half):
         if abs(step) == last:
@@ -254,11 +254,7 @@
         chip = line.chip_at(step)
         return in_ref[chip * 2 + line.core, half, :].astype(F32) + other[chip, half, :].astype(F32)
 
-    sent = {}
-    plan = [(last, 0)]
-    for k in range(last - 1, 0, -1):
-        plan += [(k, 1), (k, 0)]
-    for k, which in plan:
+    def ahead(k, which):
         for way, d in ((0, 1), (1, -1)):
             part = which if way == 0 else 1 - which
             half = halves[part]
@@ -278,6 +274,24 @@
             sent[way, k, part] = copy
             copies.append(copy)
             yield
+
+    plan = [[(last, 0)]] + [[(k, 1), (k, 0)] for k in range(last - 1, 0, -1)]
+    if paced:
+        offer(groups[0])
+        yield
+        for group, steps in zip(groups[1:], plan):
+            offer(group)
+            for step in steps:
+                for _ in ahead(*step):
+                    pass
+            yield
+    else:
+        for group in groups:
+            offer(group)
+        yield
+        for steps in plan:
+            for step in steps:
+                yield from ahead(*step)
     for part in (1, 0):
         half = halves[part]
         value = own(0, half)
@@ -308,7 +322,7 @@
     docs_ref, h_ref, mem_ref, cot_ref, wq_any, wo_any, kvw_any,
     passed_ref, gin_ref, gmem_ref, gwq_ref, gwo_ref, gself_ref, gcache_ref,
     full_h, full_s, full_c, wq, wo, kvw,
-    q_raw, kv_raw, all_kv, q_unit, dout, weights, acc, dq, attn, gq, gkv, hout,
+    q_raw, kv_raw, all_kv, q_unit, dout, weights, scores, delta_all, acc, dq, attn, gq, hout,
     proj, rows_part, source_part, dkv, part_q, part_o, part_kv, sums, mine, got,
     load, gather_send, gather_recv, pass_send, pass_recv, ex_send, ex_recv, ex_local,
     *scratch,
@@ -323,7 +337,6 @@
     rows, width = h_ref.shape
     model = width * tp
     heads = wq.shape[1] // HEAD_DIM
-    chunks = seq
 
     def cols(step):
         return pl.ds(pl.multiple_of(ring.at(step) * width, 128), width)
@@ -381,16 +394,16 @@
     own_c.wait()
     acc[...] = jnp.zeros_like(acc)
     dq[...] = jnp.zeros_like(dq)
-    low = jnp.where(is_self, jnp.maximum(me - WIN // rows, 0), 0)
-    zero_chunk = jnp.zeros((rows, 2 * HEAD_DIM), BF16)
-
-    @pl.loop(0, low)
+    low_chip = jnp.where(is_self, jnp.maximum(line.chip - WIN // (2 * rows), 0), 0)
+    zero_chunk = jnp.zeros((2 * rows, 2 * HEAD_DIM), BF16).reshape(2, rows, 2 * HEAD_DIM)
+
+    @pl.loop(0, low_chip)
     def _(j):
-        dkv[j] = zero_chunk
-
-    @pl.loop(me + 1, chunks)
+        dkv[pl.ds(2 * j, 2)] = zero_chunk
+
+    @pl.loop(line.chip + 1, line.chips)
     def _(j):
-        dkv[j] = zero_chunk
+        dkv[pl.ds(2 * j, 2)] = zero_chunk
 
     load_kvw.wait()
     next(gather_s)
@@ -425,32 +438,52 @@
         part = q_raw[:, head_cols(head)]
         unit = part * lax.rsqrt(jnp.sum(part * part, axis=1, keepdims=True) + EPS)
         q_unit[head_rows(head), :] = unit.astype(BF16)
-    next(keys)
-    next(gather_c)
-    next(keys)
-    next(keys)
-
     row = lax.broadcasted_iota(jnp.int32, (rows, 1), 0)
     lane = lax.broadcasted_iota(jnp.int32, (1, rows), 1)
     query_doc = jnp.where(row < BLK, docs_ref[0, 0], docs_ref[0, 1]).astype(F32)
     query_pos = me * rows + row
     upper = jnp.where(is_self, query_pos, query_pos // BLK * BLK + BLK - 1)
     lower = jnp.where(is_self, query_pos - WIN, -1)
-    ones = jnp.ones((rows, HEAD_DIM), BF16)
-
-    @pl.loop(low, me + 1)
-    def _(j):
-        key = all_kv[j, 0:rows, 0:HEAD_DIM]
-        value = jnp.concatenate([all_kv[j, 0:rows, HEAD_DIM:], ones], axis=1)
-        key_doc = all_kv[j, rows:, :].astype(F32)[0:1, :]
-        key_pos = j * rows + lane
-        seen = (key_doc == query_doc) & (key_pos <= upper) & (key_pos > lower)
+    ones = jnp.ones((2 * rows, HEAD_DIM), BF16)
+
+    def for_chips(hop, body):
+        count = 1 if hop % (line.chips // 2) == 0 else 2
+
+        @pl.loop(0, count)
+        def _(turn):
+            chip = line.chip_at(hop * (1 - 2 * turn))
+
+            @pl.when((chip >= low_chip) & (chip <= line.chip))
+            def _():
+                body(chip)
+
+    def forward(chip):
+        sides = [2 * chip, 2 * chip + 1]
+        value = jnp.concatenate([all_kv[j, 0:rows, HEAD_DIM:] for j in sides], axis=0)
+        value = jnp.concatenate([value, ones], axis=1)
+        seen = []
+        for j in sides:
+            key_doc = all_kv[j, rows:, :].astype(F32)[0:1, :]
+            key_pos = j * rows + lane
+            seen.append((key_doc == query_doc) & (key_pos <= upper) & (key_pos > lower))
         for head in range(heads):
-            score = nt(q_unit[head_rows(head), :], key)
-            weight = jnp.where(seen, jnp.exp2(score * EXP2_SCALE), 0.0).astype(BF16)
-            weights[j, head_rows(head), :] = weight
-            acc[head_rows(head), :] += nn(weight, value)
-
+            parts = []
+            for side, j in enumerate(sides):
+                score = nt(q_unit[head_rows(head), :], all_kv[j, 0:rows, 0:HEAD_DIM])
+                weight = jnp.where(seen[side], jnp.exp2(score * EXP2_SCALE), 0.0).astype(BF16)
+                weights[chip, head_rows(head), side * rows : (side + 1) * rows] = weight
+                parts.append(weight)
+            acc[head_rows(head), :] += nn(jnp.concatenate(parts, axis=1), value)
+
+    next(keys)
+    for_chips(0, forward)
+    next(gather_c)
+    next(keys)
+    for_chips(1, forward)
+    for_chips(2, forward)
+    next(keys)
+    for_chips(3, forward)
+    for_chips(4, forward)
     for head in range(heads):
         total = acc[head_rows(head), :]
         attn[:, head_cols(head)] = (total[:, :HEAD_DIM] * (1.0 / total[:, HEAD_DIM:])).astype(BF16)
@@ -505,32 +538,34 @@
         for _ in range(times):
             next(stream, None)
 
-    def back(start, stop):
-        @pl.loop(jnp.maximum(low, start), jnp.minimum(me + 1, stop))
-        def _(j):
-            key = all_kv[j, 0:rows, 0:HEAD_DIM]
-            value = all_kv[j, 0:rows, HEAD_DIM:]
-            grad_key = jnp.zeros((rows, HEAD_DIM), F32)
-            grad_value = jnp.zeros((rows, HEAD_DIM), F32)
-            for head in range(heads):
-                weight = weights[j, head_rows(head), :]
-                part = dout[head_rows(head), :]
-                grad_prob = nt(part, value)
-                grad_score = (weight.astype(F32) * (grad_prob - deltas[head])).astype(BF16)
-                dq[head_rows(head), :] += nn(grad_score, key)
-                grad_key += tn(grad_score, q_unit[head_rows(head), :])
-                grad_value += tn(weight, part)
-            dkv[j, :, 0:HEAD_DIM] = (SCALE * grad_key).astype(BF16)
-            dkv[j, :, HEAD_DIM:] = grad_value.astype(BF16)
-
-    quarter = chunks // 4
-    for k in range(4):
-        back(k * quarter, (k + 1) * quarter)
-        if k < 3:
+    delta_all[...] = jnp.concatenate([jnp.broadcast_to(d, (rows, 128)) for d in deltas], axis=0)
+
+    def backward(chip):
+        sides = [2 * chip, 2 * chip + 1]
+        key = jnp.concatenate([all_kv[j, 0:rows, 0:HEAD_DIM] for j in sides], axis=0)
+        for head in range(heads):
+            part = dout[head_rows(head), :]
+            delta = delta_all[head_rows(head), 0:1]
+            for side, j in enumerate(sides):
+                span = pl.ds(side * rows, rows)
+                grad_prob = nt(part, all_kv[j, 0:rows, HEAD_DIM:])
+                weight = weights[chip, head_rows(head), span].astype(F32)
+                scores[head_rows(head), span] = (weight * (grad_prob - delta)).astype(BF16)
+        dq[...] += nn(scores[...], key)
+        grad_key = (SCALE * tn(q_unit[...], scores[...])).T
+        grad_value = tn(dout[...], weights[chip]).T
+        for side, j in enumerate(sides):
+            part = slice(side * rows, (side + 1) * rows)
+            dkv[j, :, 0:HEAD_DIM] = grad_key[part].astype(BF16)
+            dkv[j, :, HEAD_DIM:] = grad_value[part].astype(BF16)
+
+    red_keys = scatter_line(line, dkv, *lines[1], finish_keys, paced=True)
+    for hop in range(line.chips // 2, -1, -1):
+        for_chips(hop, backward)
+        next(red_keys)
+        if hop:
             advance(red_hout, 2)
-            advance(red_wo, 4)
-    red_keys = scatter_line(line, dkv, *lines[1], finish_keys)
-    next(red_keys)
+            advance(red_wo, 3)
     pass_on = pass_along(sections, hout, passed_ref, pass_send, pass_recv)
     next(pass_on)
 
@@ -552,15 +587,12 @@
         rows_part[:, span] = value.astype(BF16)
     red_rows = scatter_four(ring, rows_part, *four[1], finish_input)
     next(red_rows)
-    advance(red_keys, 4)
     for k, span in enumerate(blocks):
         value = tn(full_h[:, span], scaled_q).astype(BF16)
         part_q[k * per_block : (k + 1) * per_block] = value.reshape(per_block, share, value.shape[1])
-        advance(red_keys, 1)
+        advance(red_wo, 1)
     red_wq = scatter_line(line, part_q, *lines[2], finish_wq)
-    while next(red_keys, 1) is None:
-        next(red_rows, None)
-        next(red_wo, None)
+    advance(red_keys, 2)
     next(red_wq)
     summed = sums[...]
     kv = kv_raw[...]
@@ -583,7 +615,7 @@
         next(red_wo, None)
         next(red_wq, None)
     red_kv = scatter_line(line, part_kv, *lines[3], finish_kv)
-    run_together(red_kv, red_wq, red_source, red_rows, red_wo)
+    run_together(red_kv, red_wq, red_source, red_rows, red_wo, red_keys)
 
     piece = gself_ref.shape[0]
     copies = []
@@ -634,9 +666,10 @@
         vmem((rows, cols), F32), vmem((rows, kv), F32),
         vmem((seq, rows + DOC_ROWS, kv), BF16),
         vmem((heads * rows, HEAD_DIM), BF16), vmem((heads * rows, HEAD_DIM), BF16),
-        vmem((seq, heads * rows, rows), BF16),
+        vmem((chips, heads * rows, 2 * rows), BF16),
+        vmem((heads * rows, 2 * rows), BF16), vmem((heads * rows, 128), F32),
         vmem((heads * rows, 2 * HEAD_DIM), F32), vmem((heads * rows, HEAD_DIM), F32),
-        vmem((rows, cols), BF16), vmem((rows, cols), BF16), vmem((rows, kv), BF16), vmem((rows, width), BF16),
+        vmem((rows, cols), BF16), vmem((rows, cols), BF16), vmem((rows, width), BF16),
         vmem((rows, model), BF16), vmem((rows, model), BF16), vmem((rows, model), BF16),
         vmem((seq, rows, kv), BF16),
         vmem((seq, share, cols), BF16), vmem((seq, share, cols), BF16), vmem((seq, share, kv), BF16),
@@ -666,9 +699,8 @@
 
 
 def finish_kernel(passed, gin, gmem, gwq, gwo, gself, gcache, *outs):
-    for source, target in zip((passed, gin, gmem, gwq), outs[:4]):
+    for source, target in zip((passed, gin, gmem, gwq, gwo), outs[:5]):
         target[...] = source[...]
-    outs[4][...] = gwo[...].T
     for source, target in ((gself, outs[5]), (gcache, outs[6])):
         half = source.shape[1] // 2
         target[:, 0, :] = source[:, :half]
@@ -676,8 +708,7 @@
 
 
 def finish(results):
-    shapes = [jax.ShapeDtypeStruct(x.shape, x.dtype) for x in results[:4]]
-    shapes.append(jax.ShapeDtypeStruct(results[4].shape[::-1], F32))
+    shapes = [jax.ShapeDtypeStruct(x.shape, x.dtype) for x in results[:5]]
     for x in results[5:]:
         shapes.append(jax.ShapeDtypeStruct((x.shape[0], 2, x.shape[1] // 2), F32))
     return pl.pallas_call(
@@ -699,7 +730,7 @@
         tp, seq, section, block_docs, h_in[0], memory[0], cotangent[0], w_query[0], w_out[0], kvw
     )
     passed, gin, gmem, gwq, gwo, gself, gcache = finish(results)
-    return (passed[None], gin[None], gmem[None], gwq[None], gwo[None], gself, gcache)
+    return (passed[None], gin[None], gmem[None], gwq[None], gwo.T[None], gself, gcache)
 
 
 def solution(mesh):

time: 146 us -> 134 us (0.918)
  Pallas kernels: 139 us -> 130 us
  local copies, waits for them, and re-layouts: 3.22 us -> 1.36 us
    pallas_call x1, Pallas kernels: 136 us -> 128 us  [whole_step(): pl.pallas_call(functools.partial(step_kernel, tp, seq, section), out_shap...]
    unnamed x2 -> x1, local copies, waits for them, and re-layouts: 3.22 us -> 1.36 us
where the time goes in v3:
time: 134 us
  Pallas kernels  130 us (97%)
  other arithmetic  1.58 us (1%)
  local copies, waits for them, and re-layouts  1.36 us (1%)
    pallas_call x1, Pallas kernels, whole_step(): pl.pallas_call(functools.partial(step_kernel, tp, seq, section), out_shap...  128 us

profile of v3, /device:TPU:2, one launch (start us, length us, event | category | flops | bytes accessed | tf_op | source)
XLA Modules:
  0.0 133.8 jit_solution(18150482996589541082)
XLA Ops:
  0.6 1.6 %broadcast_select_fusion = bf16[768,8,128]{2,1,0:T(8,128)(2,1)S(1)} fusion(bf16[768,8,128]{2,1,0:T(8,128)(2,1)} %bitcast.23, bf16[768,8,128]{2,1,0:T(8,128)(2,1)} %bitcast.24, pred[]{:T(512)S(6)} %eq.3), kind=kLoop, calls=%fused_computation | loop fusion | flops 786432 | bytes 4718593 | tf_op jit(solution)/shard_map/jit(_where)/select_n | solution.py:728
  2.2 1.4 %copy.17 = bf16[384,8,2,128]{3,1,2,0:T(8,128)(2,1)} copy(bf16[384,8,2,128]{3,2,1,0:T(2,128)(2,1)S(1)} %bitcast.19) | data formatting | bytes 3145728
  3.6 127.6 %step.1 = (bf16[256,768]{1,0:T(8,128)(2,1)}, bf16[256,768]{1,0:T(8,128)(2,1)}, bf16[256,768]{1,0:T(8,128)(2,1)}, f32[192,384]{1,0:T(8,128)}, f32[192,384]{1,0:T(...) custom-call(s32[1,2]{1,0:T(1,128)} %docs_ref.1, bf16[256,768]{1,0:T(8,128)(2,1)} %bitcast.25, bf16[256,768]{1,0:T(8,128)(2,1)} %bitcast.26, ...), custom_call_target="tpu_custom_call" | custom-call | tf_op jit(solution)/shard_map/step/pallas_call | solution.py:684
  131.2 2.7 %finish.1 = (bf16[256,768]{1,0:T(8,128)(2,1)}, bf16[256,768]{1,0:T(8,128)(2,1)}, bf16[256,768]{1,0:T(8,128)(2,1)}, f32[192,384]{1,0:T(8,128)}, f32[192,384]{1,0:...) custom-call(bf16[256,768]{1,0:T(8,128)(2,1)} %get-tuple-element.21.passed, ...), custom_call_target="tpu_custom_call" | custom-call | tf_op jit(solution)/shard_map/finish/pallas_call | solution.py:714

commit v4 on v3

--- a/solution.py
+++ b/solution.py
@@ -525,7 +525,6 @@
         value = tn(full_c[:, span], attn_now).astype(BF16)
         part_o[k * per_block : (k + 1) * per_block] = value.reshape(per_block, share, value.shape[1])
     red_wo = scatter_line(line, part_o, *lines[0], finish_wo)
-    next(red_wo)
     deltas = []
     for head in range(heads):
         inverse = 1.0 / acc[head_rows(head), HEAD_DIM:]
@@ -563,11 +562,9 @@
     for hop in range(line.chips // 2, -1, -1):
         for_chips(hop, backward)
         next(red_keys)
-        if hop:
+        if hop == 2:
             advance(red_hout, 2)
-            advance(red_wo, 3)
-    pass_on = pass_along(sections, hout, passed_ref, pass_send, pass_recv)
-    next(pass_on)
+    next(red_wo)
 
     total = jnp.zeros((rows, 1), F32)
     scaled = []
@@ -587,13 +584,16 @@
         rows_part[:, span] = value.astype(BF16)
     red_rows = scatter_four(ring, rows_part, *four[1], finish_input)
     next(red_rows)
+    advance(red_wo, 2)
+    advance(red_hout, 2)
+    pass_on = pass_along(sections, hout, passed_ref, pass_send, pass_recv)
+    next(pass_on)
     for k, span in enumerate(blocks):
         value = tn(full_h[:, span], scaled_q).astype(BF16)
         part_q[k * per_block : (k + 1) * per_block] = value.reshape(per_block, share, value.shape[1])
-        advance(red_wo, 1)
     red_wq = scatter_line(line, part_q, *lines[2], finish_wq)
+    next(red_wq)
     advance(red_keys, 2)
-    next(red_wq)
     summed = sums[...]
     kv = kv_raw[...]
     key, slope = kv[:, :HEAD_DIM], summed[:, :HEAD_DIM]
@@ -608,15 +608,28 @@
         source_part[:, span] = value.astype(BF16)
     red_source = scatter_four(ring, source_part, *four[2], finish_memory)
     next(red_source)
+    advance(red_wo, 4)
+    advance(red_wq, 2)
+    advance(red_rows, 2)
     scaled_kv = (both.astype(F32) * rs).astype(BF16)
     for k, span in enumerate(blocks):
         value = tn(full_s[:, span], scaled_kv).astype(BF16)
         part_kv[k * per_block : (k + 1) * per_block] = value.reshape(per_block, share, value.shape[1])
-        next(red_wo, None)
-        next(red_wq, None)
     red_kv = scatter_line(line, part_kv, *lines[3], finish_kv)
-    run_together(red_kv, red_wq, red_source, red_rows, red_wo, red_keys)
-
+    next(red_kv)
+    advance(red_wo, 4)
+    advance(red_kv, 2)
+    advance(red_wq, 4)
+    advance(red_kv, 4)
+    advance(red_wo, 4)
+    advance(red_rows, 2)
+    advance(red_wq, 4)
+    advance(red_kv, 4)
+    advance(red_source, 2)
+    advance(red_wq, 4)
+    advance(red_kv, 4)
+    advance(red_wo, 2)
+    advance(red_kv, 2)
     piece = gself_ref.shape[0]
     copies = []
     for k in range(1, section):
@@ -629,7 +642,9 @@
     first = pl.multiple_of(sections.me * piece, 8)
     local = pltpu.make_async_copy(mine.at[pl.ds(first, piece), :], got.at[sections.me], ex_local)
     local.start()
-    run_together(pass_on, red_hout, gather_s, gather_h, gather_c, keys)
+    advance(red_wq, 2)
+    run_together(red_source, pass_on, red_rows, red_hout, gather_s, gather_h, gather_c, keys)
+    run_together(red_keys, red_wo, red_wq, red_kv)
     for copy in copies:
         copy.wait_recv()
     local.wait()

time: 134 us -> 116 us (0.87)
  Pallas kernels: 130 us -> 112 us
    pallas_call x1, Pallas kernels: 128 us -> 110 us  [whole_step(): pl.pallas_call(functools.partial(step_kernel, tp, seq, section), out_shap...]
where the time goes in v4:
time: 116 us
  Pallas kernels  112 us (97%)
  other arithmetic  1.58 us (1%)
  local copies, waits for them, and re-layouts  1.36 us (1%)
    pallas_call x1, Pallas kernels, whole_step(): pl.pallas_call(functools.partial(step_kernel, tp, seq, section), out_shap...  110 us
    pallas_call x1, Pallas kernels, finish(): pl.pallas_call(finish_kernel, out_shape=tuple(shapes), in_specs=[VMEM_SPE...  2.67 us

profile of v4, /device:TPU:2, one launch (start us, length us, event | category | flops | bytes accessed | tf_op | source)
XLA Modules:
  0.0 116.1 jit_solution(8527859699419017849)
XLA Ops:
  0.6 1.6 %broadcast_select_fusion = bf16[768,8,128]{2,1,0:T(8,128)(2,1)S(1)} fusion(bf16[768,8,128]{2,1,0:T(8,128)(2,1)} %bitcast.23, bf16[768,8,128]{2,1,0:T(8,128)(2,1)} %bitcast.24, pred[]{:T(512)S(6)} %eq.3), kind=kLoop, calls=%fused_computation | loop fusion | flops 786432 | bytes 4718593 | tf_op jit(solution)/shard_map/jit(_where)/select_n | solution.py:743
  2.2 1.4 %copy.17 = bf16[384,8,2,128]{3,1,2,0:T(8,128)(2,1)} copy(bf16[384,8,2,128]{3,2,1,0:T(2,128)(2,1)S(1)} %bitcast.19) | data formatting | bytes 3145728
  3.6 109.8 %step.1 = (bf16[256,768]{1,0:T(8,128)(2,1)}, bf16[256,768]{1,0:T(8,128)(2,1)}, bf16[256,768]{1,0:T(8,128)(2,1)}, f32[192,384]{1,0:T(8,128)}, f32[192,384]{1,0:T(...) custom-call(s32[1,2]{1,0:T(1,128)} %docs_ref.1, bf16[256,768]{1,0:T(8,128)(2,1)} %bitcast.25, bf16[256,768]{1,0:T(8,128)(2,1)} %bitcast.26, ...), custom_call_target="tpu_custom_call" | custom-call | tf_op jit(solution)/shard_map/step/pallas_call | solution.py:699
  113.4 2.7 %finish.1 = (bf16[256,768]{1,0:T(8,128)(2,1)}, bf16[256,768]{1,0:T(8,128)(2,1)}, bf16[256,768]{1,0:T(8,128)(2,1)}, f32[192,384]{1,0:T(8,128)}, f32[192,384]{1,0:...) custom-call(bf16[256,768]{1,0:T(8,128)(2,1)} %get-tuple-element.21.passed, ...), custom_call_target="tpu_custom_call" | custom-call | tf_op jit(solution)/shard_map/finish/pallas_call | solution.py:729

commit v5 on v4

--- a/solution.py
+++ b/solution.py
@@ -319,9 +319,10 @@
 
 def step_kernel(
     tp, seq, section,
-    docs_ref, h_ref, mem_ref, cot_ref, wq_any, wo_any, kvw_any,
-    passed_ref, gin_ref, gmem_ref, gwq_ref, gwo_ref, gself_ref, gcache_ref,
-    full_h, full_s, full_c, wq, wo, kvw,
+    docs_ref, h_ref, mem_ref, cot_ref, wq_any, wo_any, self_any, cache_any,
+    passed_out, gin_out, gmem_out, gwq_out, gwo_out, gself_out, gcache_out,
+    passed_ref, gin_ref, gmem_ref, gwq_ref, gwo_ref, gself_ref, gcache_ref, store,
+    kv_pair, full_h, full_s, full_c, wq, wo, kvw,
     q_raw, kv_raw, all_kv, q_unit, dout, weights, scores, delta_all, acc, dq, attn, gq, hout,
     proj, rows_part, source_part, dkv, part_q, part_o, part_kv, sums, mine, got,
     load, gather_send, gather_recv, pass_send, pass_recv, ex_send, ex_recv, ex_local,
@@ -346,20 +347,23 @@
     source_self = pltpu.make_async_copy(h_ref, full_s.at[:, cols(0)], load.at[2])
     source_cross = pltpu.make_async_copy(mem_ref, full_s.at[:, cols(0)], load.at[2])
 
+    kvw_self = pltpu.make_async_copy(self_any, kv_pair, load.at[3])
+    kvw_cross = pltpu.make_async_copy(cache_any, kv_pair, load.at[3])
+
     @pl.when(is_self)
     def _():
         source_self.start()
+        kvw_self.start()
 
     @pl.when(jnp.logical_not(is_self))
     def _():
         source_cross.start()
+        kvw_cross.start()
 
     own_h.start()
     own_c.start()
-    load_kvw = pltpu.make_async_copy(kvw_any, kvw, load.at[3])
     load_wq = pltpu.make_async_copy(wq_any, wq, load.at[4])
     load_wo = pltpu.make_async_copy(wo_any, wo, load.at[5])
-    load_kvw.start()
     load_wq.start()
     load_wo.start()
     greet(
@@ -405,7 +409,14 @@
     def _(j):
         dkv[pl.ds(2 * j, 2)] = zero_chunk
 
-    load_kvw.wait()
+    kvw_self.wait()
+    pairs = 256
+
+    @pl.loop(0, model // pairs)
+    def _(k):
+        span = pl.ds(k * pairs, pairs)
+        kvw[span, :] = kv_pair[span].reshape(pairs, kvw.shape[1])
+
     next(gather_s)
     next(gather_h)
     next(gather_s)
@@ -630,6 +641,11 @@
     advance(red_kv, 4)
     advance(red_wo, 2)
     advance(red_kv, 2)
+    local_refs = (passed_ref, gin_ref, gmem_ref, gwq_ref, gwo_ref, gself_ref, gcache_ref)
+    outs = (passed_out, gin_out, gmem_out, gwq_out, gwo_out, gself_out, gcache_out)
+    stores = [pltpu.make_async_copy(a, b, store.at[k]) for k, (a, b) in enumerate(zip(local_refs, outs))]
+    stores[1].start()
+    stores[4].start()
     piece = gself_ref.shape[0]
     copies = []
     for k in range(1, section):
@@ -643,7 +659,10 @@
     local = pltpu.make_async_copy(mine.at[pl.ds(first, piece), :], got.at[sections.me], ex_local)
     local.start()
     advance(red_wq, 2)
+    stores[3].start()
     run_together(red_source, pass_on, red_rows, red_hout, gather_s, gather_h, gather_c, keys)
+    stores[0].start()
+    stores[2].start()
     run_together(red_keys, red_wo, red_wq, red_kv)
     for copy in copies:
         copy.wait_recv()
@@ -653,8 +672,12 @@
     for k in range(2, section):
         total = total + got[k]
     gcache_ref[...] = total
+    stores[5].start()
+    stores[6].start()
     for copy in copies:
         copy.wait_send()
+    for copy in stores:
+        copy.wait()
 
 
 def pass_along(ring, in_ref, out_ref, send, recv):
@@ -664,18 +687,19 @@
     copy.wait()
 
 
-def whole_step(tp, seq, section, docs, hidden, memory, cot, wq, wo, kvw):
+def whole_step(tp, seq, section, docs, hidden, memory, cot, wq, wo, self_w, cache_w):
     rows, width = hidden.shape
     model, cols = wq.shape
     heads = cols // HEAD_DIM
-    kv = kvw.shape[1]
+    kv = self_w.shape[1] * self_w.shape[2]
     chips = seq // 2
     share = model // seq
     piece = share // section
-    small = jax.ShapeDtypeStruct((rows, width), BF16)
     vmem = pltpu.VMEM
     dma = pltpu.SemaphoreType.DMA
-    scratch = [
+    outs = [((rows, width), BF16)] * 3 + [((share, cols), F32)] * 2 + [((piece, kv), F32)] * 2
+    scratch = [vmem(*out) for out in outs] + [
+        dma((7,)), vmem(self_w.shape, BF16),
         vmem((rows, model), BF16), vmem((rows, model), BF16), vmem((rows, model), BF16),
         vmem((model, cols), BF16), vmem((cols, model), BF16), vmem((model, kv), BF16),
         vmem((rows, cols), F32), vmem((rows, kv), F32),
@@ -698,28 +722,35 @@
         scratch += scatter_line_scratch(chips, *shape)
     return pl.pallas_call(
         functools.partial(step_kernel, tp, seq, section),
-        out_shape=(
-            small, small, small,
-            jax.ShapeDtypeStruct((share, cols), F32), jax.ShapeDtypeStruct((share, cols), F32),
-            jax.ShapeDtypeStruct((piece, kv), F32), jax.ShapeDtypeStruct((piece, kv), F32),
-        ),
-        in_specs=[SMEM_SPEC] + [ANY_SPEC] * 6,
-        out_specs=[VMEM_SPEC] * 7,
+        out_shape=tuple(jax.ShapeDtypeStruct(*out) for out in outs),
+        in_specs=[SMEM_SPEC] + [ANY_SPEC] * 7,
+        out_specs=[ANY_SPEC] * 7,
         scratch_shapes=scratch,
         compiler_params=pltpu.CompilerParams(
             collective_id=1, has_side_effects=True, vmem_limit_bytes=VMEM_LIMIT
         ),
         name="step",
-    )(docs, hidden, memory, cot, wq, wo, kvw)
-
-
-def finish_kernel(passed, gin, gmem, gwq, gwo, gself, gcache, *outs):
-    for source, target in zip((passed, gin, gmem, gwq, gwo), outs[:5]):
-        target[...] = source[...]
-    for source, target in ((gself, outs[5]), (gcache, outs[6])):
-        half = source.shape[1] // 2
-        target[:, 0, :] = source[:, :half]
-        target[:, 1, :] = source[:, half:]
+    )(docs, hidden, memory, cot, wq, wo, self_w, cache_w)
+
+
+def finish_kernel(passed, gin, gmem, gwq, gwo, gself, gcache, *refs):
+    outs, bufs, pair_a, pair_b, load, store = refs[:7], refs[7:14], refs[14], refs[15], refs[16], refs[17]
+    sources = (passed, gin, gmem, gwq, gwo, gself, gcache)
+    order = (5, 6, 0, 1, 2, 3, 4)
+    loads = [pltpu.make_async_copy(a, b, load.at[k]) for k, (a, b) in enumerate(zip(sources, bufs))]
+    last = bufs[:5] + (pair_a, pair_b)
+    stores = [pltpu.make_async_copy(b, a, store.at[k]) for k, (a, b) in enumerate(zip(outs, last))]
+    for k in order:
+        loads[k].start()
+    for k in order:
+        loads[k].wait()
+        if k >= 5:
+            half = bufs[k].shape[1] // 2
+            last[k][:, 0, :] = bufs[k][:, :half]
+            last[k][:, 1, :] = bufs[k][:, half:]
+        stores[k].start()
+    for copy in stores:
+        copy.wait()
 
 
 def finish(results):
@@ -729,8 +760,11 @@
     return pl.pallas_call(
         finish_kernel,
         out_shape=tuple(shapes),
-        in_specs=[VMEM_SPEC] * 7,
-        out_specs=[VMEM_SPEC] * 7,
+        in_specs=[ANY_SPEC] * 7,
+        out_specs=[ANY_SPEC] * 7,
+        scratch_shapes=[pltpu.VMEM(x.shape, x.dtype) for x in results]
+        + [pltpu.VMEM(x.shape, x.dtype) for x in shapes[5:]]
+        + [pltpu.SemaphoreType.DMA((7,)), pltpu.SemaphoreType.DMA((7,))],
         name="finish",
     )(*results)
 
@@ -738,11 +772,8 @@
 def on_device(
     tp, seq, section, h_in, memory, cotangent, block_docs, w_query, w_out, self_weight, cache_weight
 ):
-    is_self = lax.axis_index("section") == 0
-    width = w_query.shape[1]
-    kvw = jnp.where(is_self, self_weight, cache_weight).reshape(width, -1)
     results = whole_step(
-        tp, seq, section, block_docs, h_in[0], memory[0], cotangent[0], w_query[0], w_out[0], kvw
+        tp, seq, section, block_docs, h_in[0], memory[0], cotangent[0], w_query[0], w_out[0], self_weight, cache_weight
     )
     passed, gin, gmem, gwq, gwo, gself, gcache = finish(results)
     return (passed[None], gin[None], gmem[None], gwq[None], gwo.T[None], gself, gcache)

time: 116 us -> 113 us (0.974)
  other arithmetic: 1.58 us -> 0 us
  local copies, waits for them, and re-layouts: 1.36 us -> 0 us
    select_n x1 -> x0, other arithmetic: 1.58 us -> none  [on_device(): kvw = jnp.where(is_self, self_weight, cache_weight).reshape(width, -1)]
    unnamed x1 -> x0, local copies, waits for them, and re-layouts: 1.36 us -> none
where the time goes in v5:
time: 113 us; the launch traced here: 112 us
  Pallas kernels  112 us (99%)
    pallas_call x1, Pallas kernels, whole_step(): pl.pallas_call(functools.partial(step_kernel, tp, seq, section), out_shap...  109 us
    pallas_call x1, Pallas kernels, finish(): pl.pallas_call(finish_kernel, out_shape=tuple(shapes), in_specs=[ANY_SPEC...  2.38 us

profile of v5, /device:TPU:2, one launch (start us, length us, event | category | flops | bytes accessed | tf_op | source)
XLA Modules:
  0.0 112.4 jit_solution(17883486527068384392)
XLA Ops:
  0.6 109.2 %step.1 = (bf16[256,768]{1,0:T(8,128)(2,1)}, bf16[256,768]{1,0:T(8,128)(2,1)}, bf16[256,768]{1,0:T(8,128)(2,1)}, f32[192,384]{1,0:T(8,128)}, f32[192,384]{1,0:T(...) custom-call(s32[1,2]{1,0:T(1,128)} %docs_ref.1, bf16[256,768]{1,0:T(8,128)(2,1)} %bitcast.14, bf16[256,768]{1,0:T(8,128)(2,1)} %bitcast.15, ...), custom_call_target="tpu_custom_call" | custom-call | tf_op jit(solution)/shard_map/step/pallas_call | solution.py:723
  109.8 2.4 %finish.1 = (bf16[256,768]{1,0:T(8,128)(2,1)}, bf16[256,768]{1,0:T(8,128)(2,1)}, bf16[256,768]{1,0:T(8,128)(2,1)}, f32[192,384]{1,0:T(8,128)}, f32[192,384]{1,0:...) custom-call(bf16[256,768]{1,0:T(8,128)(2,1)} %get-tuple-element.21.passed, ...), custom_call_target="tpu_custom_call" | custom-call | tf_op jit(solution)/shard_map/finish/pallas_call | solution.py:760

commit v6 on v5

--- a/solution.py
+++ b/solution.py
@@ -227,7 +227,7 @@
     ]
 
 
-def scatter_line(line, in_ref, other, buf, stage, send, recv, to_core, from_core, finish, paced=False):
+def scatter_line(line, in_ref, other, buf, stage, send, recv, to_core, from_core, finish, paced=None):
     rows = in_ref.shape[1]
     last = line.chips // 2
     halves = (pl.ds(0, rows // 2), pl.ds(rows // 2, rows // 2))
@@ -276,15 +276,14 @@
             yield
 
     plan = [[(last, 0)]] + [[(k, 1), (k, 0)] for k in range(last - 1, 0, -1)]
-    if paced:
-        offer(groups[0])
+    if paced is not None:
+        paced.extend(functools.partial(offer, group) for group in groups)
         yield
-        for group, steps in zip(groups[1:], plan):
-            offer(group)
+        for steps in plan:
             for step in steps:
                 for _ in ahead(*step):
                     pass
-            yield
+                yield
     else:
         for group in groups:
             offer(group)
@@ -489,11 +488,11 @@
     next(keys)
     for_chips(0, forward)
     next(gather_c)
-    next(keys)
     for_chips(1, forward)
     for_chips(2, forward)
     next(keys)
     for_chips(3, forward)
+    next(keys)
     for_chips(4, forward)
     for head in range(heads):
         total = acc[head_rows(head), :]
@@ -530,12 +529,6 @@
     grad = nt(full_c[:, blocks[0]], wo[:, blocks[0]])
     for span in blocks[1:]:
         grad += nt(full_c[:, span], wo[:, span])
-    share = part_o.shape[1]
-    per_block = width // share
-    for k, span in enumerate(blocks):
-        value = tn(full_c[:, span], attn_now).astype(BF16)
-        part_o[k * per_block : (k + 1) * per_block] = value.reshape(per_block, share, value.shape[1])
-    red_wo = scatter_line(line, part_o, *lines[0], finish_wo)
     deltas = []
     for head in range(heads):
         inverse = 1.0 / acc[head_rows(head), HEAD_DIM:]
@@ -569,13 +562,33 @@
             dkv[j, :, 0:HEAD_DIM] = grad_key[part].astype(BF16)
             dkv[j, :, HEAD_DIM:] = grad_value[part].astype(BF16)
 
-    red_keys = scatter_line(line, dkv, *lines[1], finish_keys, paced=True)
-    for hop in range(line.chips // 2, -1, -1):
-        for_chips(hop, backward)
-        next(red_keys)
-        if hop == 2:
-            advance(red_hout, 2)
-    next(red_wo)
+    share = part_o.shape[1]
+    per_block = width // share
+
+    def weight_blocks(part, full, right, which):
+        for k in which:
+            value = tn(full[:, blocks[k]], right).astype(BF16)
+            part[k * per_block : (k + 1) * per_block] = value.reshape(per_block, share, value.shape[1])
+
+    offers = []
+    red_keys = scatter_line(line, dkv, *lines[1], finish_keys, paced=offers)
+    next(red_keys)
+    red_wo = scatter_line(line, part_o, *lines[0], finish_wo)
+    far = line.chips // 2
+    for_chips(far, backward)
+    offers[0]()
+    for_chips(far - 1, backward)
+    offers[1]()
+    next(red_keys)
+    for_chips(far - 2, backward)
+    offers[2]()
+    next(red_keys)
+    advance(red_hout, 2)
+    for_chips(far - 3, backward)
+    offers[3]()
+    next(red_keys)
+    for_chips(0, backward)
+    offers[4]()
 
     total = jnp.zeros((rows, 1), F32)
     scaled = []
@@ -589,19 +602,23 @@
         total += jnp.sum(value.astype(F32) * part, axis=1, keepdims=True)
         scaled.append((value.astype(F32) * rh).astype(BF16))
     scaled_q = jnp.concatenate(scaled, axis=1)
+    next(red_keys)
     fix = rh * rh * total / model
     for span in blocks:
         value = nt(gq[...], wq[span, :]) * rh - full_h[:, span].astype(F32) * fix
         rows_part[:, span] = value.astype(BF16)
     red_rows = scatter_four(ring, rows_part, *four[1], finish_input)
     next(red_rows)
-    advance(red_wo, 2)
+    next(red_keys)
+    weight_blocks(part_o, full_c, attn[...], range(tp))
+    next(red_wo)
+    next(red_keys)
+    next(red_keys)
     advance(red_hout, 2)
     pass_on = pass_along(sections, hout, passed_ref, pass_send, pass_recv)
     next(pass_on)
-    for k, span in enumerate(blocks):
-        value = tn(full_h[:, span], scaled_q).astype(BF16)
-        part_q[k * per_block : (k + 1) * per_block] = value.reshape(per_block, share, value.shape[1])
+    weight_blocks(part_q, full_h, scaled_q, range(tp))
+    advance(red_wo, 2)
     red_wq = scatter_line(line, part_q, *lines[2], finish_wq)
     next(red_wq)
     advance(red_keys, 2)
@@ -623,9 +640,7 @@
     advance(red_wq, 2)
     advance(red_rows, 2)
     scaled_kv = (both.astype(F32) * rs).astype(BF16)
-    for k, span in enumerate(blocks):
-        value = tn(full_s[:, span], scaled_kv).astype(BF16)
-        part_kv[k * per_block : (k + 1) * per_block] = value.reshape(per_block, share, value.shape[1])
+    weight_blocks(part_kv, full_s, scaled_kv, range(tp))
     red_kv = scatter_line(line, part_kv, *lines[3], finish_kv)
     next(red_kv)
     advance(red_wo, 4)
@@ -633,19 +648,15 @@
     advance(red_wq, 4)
     advance(red_kv, 4)
     advance(red_wo, 4)
-    advance(red_rows, 2)
+    advance(red_source, 2)
+    advance(red_kv, 4)
     advance(red_wq, 4)
     advance(red_kv, 4)
-    advance(red_source, 2)
     advance(red_wq, 4)
-    advance(red_kv, 4)
-    advance(red_wo, 2)
     advance(red_kv, 2)
     local_refs = (passed_ref, gin_ref, gmem_ref, gwq_ref, gwo_ref, gself_ref, gcache_ref)
     outs = (passed_out, gin_out, gmem_out, gwq_out, gwo_out, gself_out, gcache_out)
     stores = [pltpu.make_async_copy(a, b, store.at[k]) for k, (a, b) in enumerate(zip(local_refs, outs))]
-    stores[1].start()
-    stores[4].start()
     piece = gself_ref.shape[0]
     copies = []
     for k in range(1, section):
@@ -658,6 +669,10 @@
     first = pl.multiple_of(sections.me * piece, 8)
     local = pltpu.make_async_copy(mine.at[pl.ds(first, piece), :], got.at[sections.me], ex_local)
     local.start()
+    advance(red_wo, 2)
+    stores[4].start()
+    advance(red_rows, 2)
+    stores[1].start()
     advance(red_wq, 2)
     stores[3].start()
     run_together(red_source, pass_on, red_rows, red_hout, gather_s, gather_h, gather_c, keys)

time: 113 us -> 108 us (0.956)
  Pallas kernels: 112 us -> 107 us
    pallas_call x1, Pallas kernels: 109 us -> 104 us  [whole_step(): pl.pallas_call(functools.partial(step_kernel, tp, seq, section), out_shap...]
where the time goes in v6:
time: 108 us; the launch traced here: 107 us
  Pallas kernels  107 us (99%)
    pallas_call x1, Pallas kernels, whole_step(): pl.pallas_call(functools.partial(step_kernel, tp, seq, section), out_shap...  104 us
    pallas_call x1, Pallas kernels, finish(): pl.pallas_call(finish_kernel, out_shape=tuple(shapes), in_specs=[ANY_SPEC...  2.38 us

profile of v6, /device:TPU:2, one launch (start us, length us, event | category | flops | bytes accessed | tf_op | source)
XLA Modules:
  0.0 107.4 jit_solution(1928606562034144893)
XLA Ops:
  0.6 104.2 %step.1 = (bf16[256,768]{1,0:T(8,128)(2,1)}, bf16[256,768]{1,0:T(8,128)(2,1)}, bf16[256,768]{1,0:T(8,128)(2,1)}, f32[192,384]{1,0:T(8,128)}, f32[192,384]{1,0:T(...) custom-call(s32[1,2]{1,0:T(1,128)} %docs_ref.1, bf16[256,768]{1,0:T(8,128)(2,1)} %bitcast.14, bf16[256,768]{1,0:T(8,128)(2,1)} %bitcast.15, ...), custom_call_target="tpu_custom_call" | custom-call | tf_op jit(solution)/shard_map/step/pallas_call | solution.py:738
  104.9 2.4 %finish.1 = (bf16[256,768]{1,0:T(8,128)(2,1)}, bf16[256,768]{1,0:T(8,128)(2,1)}, bf16[256,768]{1,0:T(8,128)(2,1)}, f32[192,384]{1,0:T(8,128)}, f32[192,384]{1,0:...) custom-call(bf16[256,768]{1,0:T(8,128)(2,1)} %get-tuple-element.21.passed, ...), custom_call_target="tpu_custom_call" | custom-call | tf_op jit(solution)/shard_map/finish/pallas_call | solution.py:775
